TPU v7x, 128 devices: a whole 4x4x4 slice. The times are simulated.
128 devices in a mesh: pb: 16 (over y, x_hi, core), ka: 8 (over z, x_lo).
Axes of the slice: x: 4 (x_hi: 2, x_lo: 2; x = x_hi * 2 + x_lo), y: 4, z: 4, core: 2. Of those that a mesh axis runs over, the one named last changes fastest.
Arguments:
- bin_states: bfloat16 [8192, 1536], P(('pb', 'ka')), may hold values from -50 to 50
- contacts: int32 [8192, 16384], P('pb', 'ka'), may hold values from 0 to 2047, as said below
- w_query: bfloat16 [1536, 256], replicated, may hold values from -0.15625 to 0.15625
- w_keyval: bfloat16 [1536, 512], replicated, may hold values from -0.15625 to 0.15625
- pair_in: float32 [2, 32], replicated, may hold values from -30 to 30
- pair_shift: float32 [2, 32], replicated, may hold values from -230 to 230
- pair_out: float32 [2, 32], replicated, may hold values from -2.7 to 2.7
- w_out: bfloat16 [256, 1536], replicated, may hold values from -0.375 to 0.375
Outputs:
- mixed_out: bfloat16 [8192, 1536], P(('pb', 'ka'))
Inputs may be any that keep to these rules, and one draw needn't show every extreme that they name: contacts fall off with the distance |c - 8192|; the count at offset zero reaches 2047 in every draw.
All inputs are finite; a program needn't handle non-finite values.
Results may differ from a plain program's by a relative error of at most 0.012.
The roundings to bfloat16 on the way count: a program that leaves them out, or rounds other values in their place, can miss the bound.
Values may be sent and summed in bfloat16 or wider, within the bound.
A program may use at most 128 MiB of HBM per device.

v0:
```python
import jax
import jax.numpy as jnp
from jax import lax
from jax.sharding import PartitionSpec as P

HEADS = 2
HEAD_DIM = 128
PAIR_HIDDEN = 32
HALF_BAND = 8192


def shifted(block, axis, distance):
    devices = range(lax.axis_size(axis))
    route = [((i - distance) % len(devices), i) for i in devices]
    return lax.ppermute(block, axis, route)


def shear_rows(tile):
    leading, height, length = tile.shape
    padded = jnp.pad(tile, ((0, 0), (0, 0), (0, height + 1)))
    flattened = padded.reshape(leading, height * (length + height + 1))
    flattened = flattened[:, : height * (length + height)]
    return flattened.reshape(leading, height, length + height)


def pair_bias(pair_counts, pair_in, pair_shift, pair_out):
    log_counts = jnp.log(1.0 + pair_counts.astype(jnp.float32))
    per_head = []
    for head_index in range(HEADS):
        summed = jnp.zeros(log_counts.shape, jnp.float32)
        for hidden_unit in range(PAIR_HIDDEN):
            inner = (
                pair_in[head_index, hidden_unit] * log_counts + pair_shift[head_index, hidden_unit]
            )
            summed = summed + pair_out[head_index, hidden_unit] * jax.nn.silu(inner)
        per_head.append(summed)
    return jnp.stack(per_head, 0)


def shards(bin_states, contacts, w_query, w_keyval, pair_in, pair_shift, pair_out, w_out):
    head_cols = HEADS * HEAD_DIM
    queries = jnp.dot(bin_states, w_query, preferred_element_type=jnp.float32).astype(jnp.bfloat16)
    key_values = jnp.dot(bin_states, w_keyval, preferred_element_type=jnp.float32).astype(
        jnp.bfloat16
    )
    query_block, keyval_block = (
        lax.all_gather(queries, "ka", axis=0, tiled=True),
        lax.all_gather(key_values, "ka", axis=0, tiled=True),
    )
    pb_count = lax.axis_size("pb")
    ka_count = lax.axis_size("ka")
    pb_index = lax.axis_index("pb")
    ka_index = lax.axis_index("ka")
    query_rows = query_block.shape[0]
    offsets = contacts.shape[1]
    span_ratio = offsets // query_rows
    lead_blocks = HALF_BAND // query_rows
    seq_len = query_rows * pb_count
    key_start = pb_index * query_rows + ka_index * offsets - HALF_BAND
    pieces = []
    for step_index in range(span_ratio + 1):
        amount = (lead_blocks - step_index) % pb_count
        if amount == 0:
            pieces.append(keyval_block)
        else:
            pieces.append(shifted(keyval_block, "pb", amount))
    key_window = jnp.concatenate(pieces, 0)
    for bit_pos in range(ka_count.bit_length() - 1):
        amount = -(span_ratio << bit_pos) % pb_count
        if amount != 0:
            arrived = shifted(key_window, "pb", amount)
            key_window = jnp.where(ka_index >> bit_pos & 1 == 1, arrived, key_window)
    sub_rows = min(512, query_rows)
    sub_count = query_rows // sub_rows
    key_span = sub_rows + offsets
    inv_root = 1.0 / HEAD_DIM**0.5
    row_pos = jnp.arange(sub_rows, dtype=jnp.int32)[:, None]
    col_pos = jnp.arange(key_span, dtype=jnp.int32)[None, :]

    def score_block(block_index):
        first_row = block_index * sub_rows
        rows_query = query_block.reshape(sub_rows, HEADS, HEAD_DIM)
        keys_here = key_window[:, :head_cols]
        key_heads = keys_here.reshape(key_span, HEADS, HEAD_DIM)
        bias_tile = shear_rows(pair_bias(contacts, pair_in, pair_shift, pair_out))
        scores = (
            jnp.einsum("ihd,khd->hik", rows_query, key_heads, preferred_element_type=jnp.float32)
            * inv_root
            + bias_tile
        )
        key_pos = key_start + first_row + col_pos
        allowed = (
            (col_pos >= row_pos)
            & (col_pos < row_pos + offsets)
            & (key_pos >= 0)
            & (key_pos < seq_len)
        )
        return jnp.where(allowed[None], scores, -1e30)

    block_ids = jnp.arange(sub_count, dtype=jnp.int32)
    scores = lax.map(score_block, block_ids)
    row_top = lax.pmax(jnp.max(scores, axis=3), "ka")

    def weigh_block(operands):
        block_scores, block_top, block_index = operands
        weights = jnp.exp(block_scores - block_top[:, :, None]).astype(jnp.bfloat16)
        totals = jnp.sum(weights, axis=2, dtype=jnp.float32)
        values_here = key_window[:, head_cols:]
        value_heads = values_here.reshape(key_span, HEADS, HEAD_DIM)
        numerators = jnp.einsum(
            "hik,khd->ihd", weights, value_heads, preferred_element_type=jnp.float32
        )
        return (numerators.reshape(sub_rows, head_cols), jnp.transpose(totals))

    numerators, totals = lax.map(weigh_block, (scores, row_top, block_ids))
    numerators = numerators.reshape(query_rows, head_cols)
    totals = totals.reshape(query_rows, HEADS)
    share_rows = query_rows // ka_count
    summed_num, summed_tot = lax.psum((numerators, totals), "ka")
    first_share = ka_index * share_rows
    summed_num = lax.dynamic_slice_in_dim(summed_num, first_share, share_rows, 0)
    summed_tot = lax.dynamic_slice_in_dim(summed_tot, first_share, share_rows, 0)
    attended = summed_num.reshape(share_rows, HEADS, HEAD_DIM) / summed_tot[:, :, None]
    attended = attended.reshape(share_rows, head_cols).astype(jnp.bfloat16)
    return jnp.dot(attended, w_out, preferred_element_type=jnp.float32).astype(jnp.bfloat16)


def solution(mesh):
    placed = (P(("pb", "ka"), None), P("pb", "ka"), P(), P(), P(), P(), P(), P())
    return jax.shard_map(
        shards, mesh=mesh, in_specs=placed, out_specs=P(("pb", "ka"), None), check_vma=False
    )
```

profile of v0, /device:TPU:16, one launch (start us, length us, event | category | flops | bytes accessed | tf_op | source)
XLA Modules:
  0.0 525.4 jit_solution(3791947021305828865)
XLA Ops:
  6.5 1.4 copy-done
  7.9 1.5 convolution_convert_fusion.1
  9.4 31.3 %all_gather.6 = bf16[512,512]{1,0:T(8,128)(2,1)S(1)} all-gather(bf16[64,512]{1,0:T(8,128)(2,1)S(1)} %convolution_convert_fusion.1), channel_id=1, replica_groups=mesh['pb'=16,'ka'=8] {'ka'}, dimensions={0}, use_global_device_ids=true | all-gather | bytes 589824 | tf_op jit(solution)/shard_map/all_gather | solution.py:48
  40.7 2.8 collective-permute-start.1
  43.8 3.0 collective-permute-start.3
  46.8 2.1 fusion.14
  49.0 2.1 fusion.17
  51.1 2.1 fusion.13
  53.1 2.1 fusion.16
  55.2 2.1 fusion.12
  57.3 2.1 fusion.15
  59.4 1.6 fusion.23
  61.1 1.6 fusion.22
  62.7 1.6 fusion.21
  66.0 1.6 collective-permute-done.1
  70.5 113.2 %add_bitcast_fusion = f32[1,512,2048]{2,1,0:T(8,128)} fusion(s32[512,2048]{1,0:T(8,128)S(1)} %copy-done.9, f32[]{:T(128)} %bitcast.193, f32[]{:T(128)} %bitcast.192, f32[]{:T(128)} %bitcast.191, f32[]{:T(128)} %bitcast.190, f32[]{:T(128)} %bitcast.189, f32[]{:T(128)} %bitcast.188, f32[]{:T(128)} %bitcast.187, f32[]{:T(128)} %bitcast.186, f32[]{:T(128)} %bitcast.185, ...), kind=kLoop, calls=%fused_computation.11 | loop fusion | flops 269484032 | bytes 8388992 | tf_op jit(solution)/shard_map/while/body/eval_jaxpr/stack | solution.py:37
  185.8 3.6 broadcast_select_fusion
  189.4 2.9 collective-permute-start.5
  192.3 112.8 %add_bitcast_fusion.1 = f32[1,512,2048]{2,1,0:T(8,128)} fusion(s32[512,2048]{1,0:T(8,128)S(1)} %copy-done.10, f32[]{:T(128)} %bitcast.96, f32[]{:T(128)} %bitcast.95, f32[]{:T(128)} %bitcast.94, f32[]{:T(128)} %bitcast.93, f32[]{:T(128)} %bitcast.92, f32[]{:T(128)} %bitcast.91, f32[]{:T(128)} %bitcast.90, f32[]{:T(128)} %bitcast.89, f32[]{:T(128)} %bitcast.88, ...), kind=kLoop, calls=%fused_computation.12 | loop fusion | flops 269484032 | bytes 8388992 | tf_op jit(solution)/shard_map/while/body/eval_jaxpr/stack | solution.py:37
  305.1 8.5 %select_maximum_fusion = f32[2,512,2561]{2,1,0:T(8,128)} fusion(f32[1,512,2048]{2,1,0:T(8,128)} %add_bitcast_fusion, f32[1,512,2048]{2,1,0:T(8,128)} %add_bitcast_fusion.1), kind=kLoop, calls=%fused_computation | loop fusion | flops 10489856 | bytes 18878464 | tf_op jit(solution)/shard_map/while/body/eval_jaxpr/stack | solution.py:37
  313.7 15.9 %reshape.122 = f32[2622464]{0:T(1024)} reshape(f32[2,512,2561]{2,1,0:T(8,128)} %select_maximum_fusion) | data formatting | bytes 20979712
  329.6 16.6 %reshape.118 = f32[2,1311232]{1,0:T(2,128)} reshape(f32[2622464]{0:T(1024)} %reshape.122) | data formatting | bytes 20979712 | tf_op jit(solution)/shard_map/while/body/eval_jaxpr/reshape | solution.py:21
  346.2 8.5 %slice.977 = f32[2,1310720]{1,0:T(2,128)} slice(f32[2,1311232]{1,0:T(2,128)} %reshape.118), slice={[0:2], [0:1310720]} | slice | bytes 20971520 | tf_op jit(solution)/shard_map/while/body/eval_jaxpr/slice | solution.py:22
  355.0 28.7 %all_gather.7 = bf16[512,256]{1,0:T(8,128)(2,1)S(1)} all-gather(bf16[64,256]{1,0:T(8,128)(2,1)S(1)} %convolution_convert_fusion.2), channel_id=1, replica_groups=mesh['pb'=16,'ka'=8] {'ka'}, dimensions={0}, use_global_device_ids=true | all-gather | bytes 294912 | tf_op jit(solution)/shard_map/all_gather | solution.py:47
  385.1 2.0 broadcast_select_fusion.1
  388.5 1.6 copy.15
  390.0 10.8 %fusion.24 = (f32[2,512]{1,0:T(2,128)S(1)}, f32[2,512,2560]{2,1,0:T(8,128)}) fusion(f32[1,2,512,2560]{3,1,2,0:T(2,128)} %bitcast.233, bf16[320,2,8,128]{3,2,1,0:T(8,128)(2,1)} %get-tuple-element.31, pred[512,2560]{1,0:T(8,128)(4,1)S(1)} %fusion.3, bf16[512,256]{1,0:T(8,128)(2,1)S(1)} %all_gather.7), kind=kOutput, calls=%fused_computation.49 | convolution fusion | flops 681573376 | bytes 23859200 | tf_op jit(solution)/shard_map/while/body/eval_jaxpr/ihd,khd->hik/dot_general | solution.py:87
  400.8 18.4 %pmax.7 = f32[2,512]{1,0:T(2,128)S(1)} all-reduce(f32[2,512]{1,0:T(2,128)S(1)} %get-tuple-element.250), channel_id=1, replica_groups=mesh['pb'=16,'ka'=8] {'ka'}, use_global_device_ids=true, to_apply=%region_1.2 | all-reduce | flops 1024 | bytes 8192 | tf_op jit(solution)/shard_map/pmax | solution.py:102
  419.2 6.7 %fusion.4 = f32[2,128,512]{2,1,0:T(8,128)} fusion(bf16[2560,2,128]{0,2,1:T(8,128)(2,1)S(1)} %bitcast.234, f32[2,512,2560]{2,1,0:T(8,128)} %get-tuple-element.251, f32[2,512]{1,0:T(2,128)S(1)} %pmax.7), kind=kOutput, calls=%fused_computation.17 | convolution fusion | flops 676331520 | bytes 12324864 | tf_op jit(solution)/shard_map/while/body/eval_jaxpr/hik,khd->ihd/dot_general | solution.py:110
  426.0 5.6 %convert_reduce_fusion = f32[2,512]{1,0:T(2,128)S(1)} fusion(f32[2,512,2560]{2,1,0:T(8,128)} %get-tuple-element.251, f32[2,512]{1,0:T(2,128)S(1)} %pmax.7), kind=kLoop, calls=%fused_computation.4 | loop fusion | flops 10484736 | bytes 10493952 | tf_op jit(solution)/shard_map/while/body/eval_jaxpr/reduce_sum | solution.py:107
  431.6 16.0 %psum.15 = f32[512,2]{0,1:T(2,128)S(1)} all-reduce(f32[512,2]{0,1:T(2,128)S(1)} %bitcast.236), channel_id=1, replica_groups=mesh['pb'=16,'ka'=8] {'ka'}, use_global_device_ids=true, to_apply=%region_4.5 | all-reduce | flops 1024 | bytes 8192 | tf_op jit(solution)/shard_map/psum | solution.py:119
  447.7 68.8 %all-reduce.3.cloned.1.call-done = f32[512,256]{0,1:T(8,128)} async-done(((f32[512,256]{0,1:T(8,128)}), f32[512,256]{0,1:T(8,128)}) %all-reduce.3.cloned.1.call-update) | async-done | bytes 524304 | tf_op jit(solution)/shard_map/psum | solution.py:119
  (47 shorter events, 12.2 us)
Async XLA Ops:
  6.5 1.4 copy-start
  6.5 510.0 %all-reduce.3.cloned.1.call-start = ((), (), s32[]{:S(2)}) async-start(), calls=%async_computation | async-start | bytes 1048576 | tf_op jit(solution)/shard_map/psum | solution.py:119
  7.9 62.5 %copy-start.9 = (s32[512,2048]{1,0:T(8,128)S(1)}, s32[512,2048]{1,0:T(8,128)}, u32[]{:S(2)}) copy-start(s32[512,2048]{1,0:T(8,128)} %param.9) | copy-start | bytes 12582916
  40.7 24.4 %collective-permute-start = (bf16[512,512]{1,0:T(8,128)(2,1)S(1)}, bf16[512,512]{1,0:T(8,128)(2,1)S(1)}, u32[]{:S(2)}, u32[]{:S(2)}) collective-permute-start(bf16[512,512]{1,0:T(8,128)(2,1)S(1)} %all_gather.6), channel_id=1, source_target_pairs={{8,0},{16,8},{24,16},{32,24},{40,32},{48,40},{56,48},{64,56},{72,6... | collective-permute-start | bytes 1572872 | tf_op jit(solution)/shard_map/ppermute | solution.py:15
  40.7 26.8 %collective-permute-start.1 = (bf16[512,512]{1,0:T(8,128)(2,1)S(1)}, bf16[512,512]{1,0:T(8,128)(2,1)S(1)}, u32[]{:S(2)}, u32[]{:S(2)}) collective-permute-start(bf16[512,512]{1,0:T(8,128)(2,1)S(1)} %all_gather.6), channel_id=1, source_target_pairs={{16,0},{24,8},{32,16},{40,24},{48,32},{56,40},{64,48},{72,56},{80,... | collective-permute-start | bytes 1572872 | tf_op jit(solution)/shard_map/ppermute | solution.py:15
  43.6 24.8 %collective-permute-start.2 = (bf16[512,512]{1,0:T(8,128)(2,1)S(1)}, bf16[512,512]{1,0:T(8,128)(2,1)S(1)}, u32[]{:S(2)}, u32[]{:S(2)}) collective-permute-start(bf16[512,512]{1,0:T(8,128)(2,1)S(1)} %all_gather.6), channel_id=1, source_target_pairs={{24,0},{32,8},{40,16},{48,24},{56,32},{64,40},{72,48},{80,56},{88,... | collective-permute-start | bytes 1572872 | tf_op jit(solution)/shard_map/ppermute | solution.py:15
  43.8 25.4 %collective-permute-start.3 = (bf16[512,512]{1,0:T(8,128)(2,1)S(1)}, bf16[512,512]{1,0:T(8,128)(2,1)S(1)}, u32[]{:S(2)}, u32[]{:S(2)}) collective-permute-start(bf16[512,512]{1,0:T(8,128)(2,1)S(1)} %all_gather.6), channel_id=1, source_target_pairs={{32,0},{40,8},{48,16},{56,24},{64,32},{72,40},{80,48},{88,56},{96,... | collective-permute-start | bytes 1572872 | tf_op jit(solution)/shard_map/ppermute | solution.py:15
  70.0 115.8 %collective-permute-start.4 = (bf16[2560,512]{1,0:T(8,128)(2,1)}, bf16[2560,512]{1,0:T(8,128)(2,1)}, u32[]{:S(2)}, u32[]{:S(2)}) collective-permute-start(bf16[2560,512]{1,0:T(8,128)(2,1)} %constant_dynamic-update-slice_fusion), channel_id=1, source_target_pairs={{32,0},{40,8},{48,16},{56,24},{64,32},{72,40},{80,48},{88,56},{96,... | collective-permute-start | bytes 7864328 | tf_op jit(solution)/shard_map/ppermute | solution.py:15
  70.5 113.2 %copy-start.3 = (f32[2,32]{1,0:T(2,128)S(1)}, f32[2,32]{1,0:T(2,128)}, u32[]{:S(2)}) copy-start(f32[2,32]{1,0:T(2,128)} %param.13) | copy-start | bytes 772
  70.5 113.9 %copy-start.4 = (f32[2,32]{1,0:T(2,128)S(1)}, f32[2,32]{1,0:T(2,128)}, u32[]{:S(2)}) copy-start(f32[2,32]{1,0:T(2,128)} %param.12) | copy-start | bytes 772
  70.5 114.6 %copy-start.5 = (f32[2,32]{1,0:T(2,128)S(1)}, f32[2,32]{1,0:T(2,128)}, u32[]{:S(2)}) copy-start(f32[2,32]{1,0:T(2,128)} %param.14) | copy-start | bytes 772
  183.7 8.7 %copy-start.10 = (s32[512,2048]{1,0:T(8,128)S(1)}, s32[512,2048]{1,0:T(8,128)}, u32[]{:S(2)}) copy-start(s32[512,2048]{1,0:T(8,128)} %param.9) | copy-start | bytes 12582916
  189.4 195.6 %collective-permute-start.5 = (bf16[2560,512]{1,0:T(8,128)(2,1)}, bf16[2560,512]{1,0:T(8,128)(2,1)}, u32[]{:S(2)}, u32[]{:S(2)}) collective-permute-start(bf16[2560,512]{1,0:T(8,128)(2,1)} %broadcast_select_fusion), channel_id=1, source_target_pairs={{64,0},{72,8},{80,16},{88,24},{96,32},{104,40},{112,48},{120,56},{... | collective-permute-start | bytes 7864328 | tf_op jit(solution)/shard_map/ppermute | solution.py:15
  346.2 8.6 %copy-start.7 = (bf16[1536,256]{1,0:T(8,128)(2,1)S(1)}, bf16[1536,256]{1,0:T(8,128)(2,1)}, u32[]{:S(2)}) copy-start(bf16[1536,256]{1,0:T(8,128)(2,1)} %param.10) | copy-start | bytes 2359300
  346.2 8.6 %copy-start.8 = (bf16[64,1536]{1,0:T(8,128)(2,1)S(1)}, bf16[64,1536]{1,0:T(8,128)(2,1)}, u32[]{:S(2)}) copy-start(bf16[64,1536]{1,0:T(8,128)(2,1)} %param.8) | copy-start | bytes 589828
  390.0 29.1 %copy-start.2 = (bf16[2560,256]{0,1:T(8,128)(2,1)S(1)}, bf16[2560,256]{0,1:T(8,128)(2,1)}, u32[]{:S(2)}) copy-start(bf16[2560,256]{0,1:T(8,128)(2,1)} %copy.15) | copy-start | bytes 3932164
  425.9 91.6 %copy-start.6 = (bf16[256,1536]{1,0:T(8,128)(2,1)S(1)}, bf16[256,1536]{1,0:T(8,128)(2,1)}, u32[]{:S(2)}) copy-start(bf16[256,1536]{1,0:T(8,128)(2,1)} %param.15) | copy-start | bytes 2359300
  425.9 92.6 %copy-start.1 = (bf16[1536,512]{1,0:T(8,128)(2,1)S(1)}, bf16[1536,512]{1,0:T(8,128)(2,1)}, u32[]{:S(2)}) copy-start(bf16[1536,512]{1,0:T(8,128)(2,1)} %param.11) | copy-start | bytes 4718596
Sparse Core Ops, SparseCore 0:
  426.0 90.4 all-reduce.2
where the time goes:
time: 528 us; the launch traced here: 525 us
  other arithmetic  248 us (47%)
  blocking collectives  94.4 us (18%)
  waiting for transfers between devices  70.4 us (13%)
  local copies, waits for them, and re-layouts  69.3 us (13%)
  matrix products  20.2 us (4%)
  between operations  13.5 us (3%)
  starting transfers between devices  9.46 us (2%)
    another operation x3, other arithmetic, pair_bias(): return jnp.stack(per_head, 0)  234 us
    psum x1, waiting for transfers between devices, shards(): summed_num, summed_tot = lax.psum((numerators, totals), 'ka')  68.8 us
    all_gather x1, blocking collectives, shards(): lax.all_gather(key_values, 'ka', axis=0, tiled=True)  31.3 us
    all_gather x1, blocking collectives, shards(): lax.all_gather(queries, 'ka', axis=0, tiled=True)  28.7 us
    unnamed x28, local copies, waits for them, and re-layouts  22.1 us
    pmax x1, blocking collectives, shards(): row_top = lax.pmax(jnp.max(scores, axis=3), 'ka')  18.4 us
    reshape x1, local copies, waits for them, and re-layouts, shear_rows(): flattened = padded.reshape(leading, height * (length + height + 1))  16.6 us
    psum x1, blocking collectives, shards(): summed_num, summed_tot = lax.psum((numerators, totals), 'ka')  16 us
  transfers between devices with their start and end apart: 7, of which 2 were waited for; matrix products, arithmetic and copies ran while one was open for 58% of the time, Pallas kernels for 0%

commit v1 on v0

v1 whole, which is shorter than its diff:
```python
import functools
import jax
import jax.numpy as jnp
from jax import lax
from jax.experimental import pallas as pl
from jax.experimental.pallas import tpu as pltpu
from jax.sharding import PartitionSpec as P

HEADS = 2
HEAD_DIM = 128
PAIR_HIDDEN = 32
HALF_BAND = 8192
SEGS = 16
ROOT = HEAD_DIM**0.5
LOG2E = 1.4426950408889634
NEG = -1e30
MESH = pl.DeviceIdType.MESH
F32 = jnp.float32
BF16 = jnp.bfloat16


def gather_kernel(
    pbn, kan, x_ref, wq_ref, wkv_ref, q_out, win_out,
    qs, kvs, q_send, q_recv, kv_send, kv_recv, f_send, f_recv,
):
    p = lax.axis_index("pb")
    k = lax.axis_index("ka")
    rows = x_ref.shape[0]
    block = rows * kan
    partner = p + 1 - 2 * (p % 2)
    first = p + 4 * k - 16

    def dest(kd, m):
        pd = p - 4 * kd + 16 - 2 * m
        return pd, (pd >= 0) & (pd < pbn)

    def has(m):
        b = first + 2 * m
        return (b >= 0) & (b < pbn)

    barrier = pltpu.get_barrier_semaphore()
    for i in range(1, kan):
        pl.semaphore_signal(
            barrier, inc=1, device_id=(p, lax.rem(k + i, kan)), device_id_type=MESH
        )
    pl.semaphore_signal(barrier, inc=1, device_id=(partner, k), device_id_type=MESH)
    for m in range(3):
        b = first + 2 * m
        for i in range(kan):
            own = (b == p) & (i == 0)

            @pl.when(has(m) & jnp.logical_not(own))
            def _(b=b, i=i):
                pl.semaphore_signal(
                    barrier, inc=1, device_id=(b, lax.rem(k + i, kan)), device_id_type=MESH
                )

    qs[...] = jnp.dot(x_ref[...], wq_ref[...], preferred_element_type=F32).astype(BF16)
    kvs[...] = jnp.dot(x_ref[...], wkv_ref[...], preferred_element_type=F32).astype(BF16)

    expected = kan
    for i in range(kan):
        kd = lax.rem(k + i, kan)
        for m in range(3):
            pd, ok = dest(kd, m)
            own = (pd == p) & (i == 0)
            expected = expected + jnp.where(ok & jnp.logical_not(own), 1, 0)
    pl.semaphore_wait(barrier, expected)

    def q_copy(i):
        kd = lax.rem(k + i, kan)
        return pltpu.make_async_remote_copy(
            src_ref=qs, dst_ref=q_out.at[pl.ds(k * rows, rows)],
            send_sem=q_send.at[i], recv_sem=q_recv,
            device_id=(p, kd), device_id_type=MESH,
        )

    def kv_rows(m):
        return win_out.at[pl.ds(2 * m * block + k * rows, rows)]

    def kv_copy(i, m, pd, kd):
        return pltpu.make_async_remote_copy(
            src_ref=kvs, dst_ref=kv_rows(m),
            send_sem=kv_send.at[i, m], recv_sem=kv_recv.at[m],
            device_id=(pd, kd), device_id_type=MESH,
        )

    for i in range(kan):
        kd = lax.rem(k + i, kan)
        for m in range(3):
            pd, ok = dest(kd, m)
            own = (pd == p) & (i == 0)

            @pl.when(ok & jnp.logical_not(own))
            def _(i=i, m=m, pd=pd, kd=kd):
                kv_copy(i, m, pd, kd).start()

            if i == 0:

                @pl.when(ok & own)
                def _(m=m):
                    pltpu.make_async_copy(kvs, kv_rows(m), kv_recv.at[m]).start()

        if i:
            q_copy(i).start()
    own_q = pltpu.make_async_copy(qs, q_out.at[pl.ds(k * rows, rows)], q_recv)
    own_q.start()

    odd = p % 2

    def fwd(slot):
        m = slot + 1 - odd
        return pltpu.make_async_remote_copy(
            src_ref=win_out.at[pl.ds(2 * m * block, block)],
            dst_ref=win_out.at[pl.ds((2 * slot + 1) * block, block)],
            send_sem=f_send.at[slot], recv_sem=f_recv.at[slot],
            device_id=(partner, k), device_id_type=MESH,
        )

    def in_block(m):
        part = win_out.at[pl.ds(2 * m * block, block)]
        return pltpu.make_async_remote_copy(
            src_ref=part, dst_ref=part, send_sem=kv_send.at[0, m], recv_sem=kv_recv.at[m],
            device_id=(partner, k), device_id_type=MESH,
        )

    for m in range(3):

        @pl.when(has(m))
        def _(m=m):
            in_block(m).wait_recv()

        for slot in range(2):
            b = first + 2 * m

            @pl.when(has(m) & (slot + 1 - odd == m))
            def _(slot=slot):
                fwd(slot).start()

    for slot in range(2):
        b_in = first + 2 * slot + 1

        @pl.when((b_in >= 0) & (b_in < pbn))
        def _(slot=slot):
            fwd(slot).wait_recv()

        b_out = first + 2 * (slot + 1 - odd)

        @pl.when((b_out >= 0) & (b_out < pbn))
        def _(slot=slot):
            fwd(slot).wait_send()

    for i in range(kan):
        kd = lax.rem(k + i, kan)
        for m in range(3):
            pd, ok = dest(kd, m)
            own = (pd == p) & (i == 0)

            @pl.when(ok & jnp.logical_not(own))
            def _(i=i, m=m, pd=pd, kd=kd):
                kv_copy(i, m, pd, kd).wait_send()

        if i:
            q_copy(i).wait_send()
    whole = pltpu.make_async_remote_copy(
        src_ref=q_out, dst_ref=q_out, send_sem=q_send.at[0], recv_sem=q_recv,
        device_id=(partner, k), device_id_type=MESH,
    )
    whole.wait_recv()


def attend_kernel(
    tiles, blocks, start_ref, pin_ref, psh_ref, pout_ref, con_ref, q_ref, win_ref, msg_ref,
    tab, bias, smax, sbuf, acc, seen, fix,
):
    rb = pl.program_id(0)
    first = start_ref[0]
    lanes = lax.broadcasted_iota(jnp.int32, (128, 128), 1)
    subl = lax.broadcasted_iota(jnp.int32, (128, 128), 0)
    here = lanes >= subl
    pad = 4

    @pl.when(rb == 0)
    def _():
        ids = (
            lax.broadcasted_iota(jnp.int32, (SEGS, 128), 0) * 128
            + lax.broadcasted_iota(jnp.int32, (SEGS, 128), 1)
        )
        logc = jnp.log(1.0 + ids.astype(F32))
        for h in range(HEADS):
            summed = jnp.zeros((SEGS, 128), F32)
            for u in range(PAIR_HIDDEN):
                inner = pin_ref[h, u] * logc + psh_ref[h, u]
                summed = summed + pout_ref[h, u] * (inner / (1.0 + jnp.exp(-inner)))
            summed = summed * ROOT
            for s in range(SEGS):
                tab[h, s] = jnp.broadcast_to(summed[s : s + 1], (8, 128))
            bias[h, :, 0 : pad * 128] = jnp.full((128, pad * 128), NEG, F32)
            bias[h, :, (pad + tiles) * 128 : (2 * pad + tiles) * 128] = jnp.full(
                (128, pad * 128), NEG, F32
            )

    lo = jnp.maximum(0, -first)
    hi = jnp.minimum(tiles // 4 + 1, blocks - first)
    active = hi > lo

    smax[...] = jnp.full(smax.shape, NEG, F32)
    acc[...] = jnp.zeros(acc.shape, F32)

    def pick(table, low):
        dims = lax.GatherDimensionNumbers(
            offset_dims=(), collapsed_slice_dims=(1,), start_index_map=(1,),
            operand_batching_dims=(0,), start_indices_batching_dims=(0,),
        )
        return lax.gather(
            table, low[:, :, None], dims, slice_sizes=(1, 1),
            mode=lax.GatherScatterMode.PROMISE_IN_BOUNDS,
        )

    def roll(x):
        return pltpu.roll(x, 0, 1, stride=1, stride_axis=0)

    @pl.when(active)
    def _():
        tables = [tab[h, 0] for h in range(HEADS)]

        def look(it, every):
            for u in range(4):
                at = pl.multiple_of((it * 4 + u) * 128, 128)
                c = con_ref[:, pl.ds(at, 128)]
                some = functools.reduce(
                    jnp.bitwise_or, [c[8 * g : 8 * g + 8] for g in range(16)]
                )
                seen[it * 4 + u] = some
                every = every | some
                low = roll(c & 127)
                for g in range(16):
                    for h in range(HEADS):
                        bias[h, 8 * g : 8 * g + 8, pl.ds(at + pad * 128, 128)] = pick(
                            tables[h], low[8 * g : 8 * g + 8]
                        )
            return every

        every = lax.fori_loop(0, tiles // 4, look, jnp.zeros((8, 128), jnp.int32))

        @pl.when(jnp.max(every.astype(F32)) > 127.5)
        def _():
            def tile(j, _):
                most = jnp.max(seen[j].astype(F32))

                @pl.when(most > 127.5)
                def _():
                    at = pl.multiple_of(j * 128, 128)
                    fix[...] = jnp.zeros(fix.shape, F32)
                    rounds = (most.astype(jnp.int32) >> 9) + 1

                    def some_rows(r, _):
                        for g in range(16):
                            c = con_ref[8 * g : 8 * g + 8, pl.ds(at, 128)]
                            low = c & 127
                            row = c >> 7
                            for h in range(HEADS):
                                got = fix[h, 8 * g : 8 * g + 8]
                                for u in range(4):
                                    got = jnp.where(
                                        row == 4 * r + u, pick(tab[h, 4 * r + u], low), got
                                    )
                                fix[h, 8 * g : 8 * g + 8] = got
                        return 0

                    lax.fori_loop(0, rounds, some_rows, 0)
                    for h in range(HEADS):
                        bias[h, :, pl.ds(at + pad * 128, 128)] = roll(fix[h])

                return 0

            lax.fori_loop(0, tiles, tile, 0)

        q = q_ref[...]

        def score(j, _):
            for h in range(HEADS):
                keys = win_ref[
                    pl.ds(pl.multiple_of(j * 512, 512), 512), 128 * h : 128 * h + 128
                ]
                s = jnp.dot(q[:, 128 * h : 128 * h + 128], keys.T, preferred_element_type=F32)
                top = smax[h]
                for i in range(4):
                    at = pl.multiple_of((pad + 4 * j + i - rb) * 128, 128)
                    b = jnp.where(here, bias[h, :, pl.ds(at, 128)], bias[h, :, pl.ds(at - 128, 128)])
                    part = s[:, 128 * i : 128 * i + 128] + b
                    sbuf[h, :, pl.ds(pl.multiple_of((4 * j + i) * 128, 128), 128)] = part
                    top = jnp.maximum(top, part)
                smax[h] = top
            return 0

        lax.fori_loop(lo, hi, score, 0)
        for h in range(HEADS):
            smax[h] = jnp.broadcast_to(jnp.max(smax[h], axis=1, keepdims=True), (128, 128))
        ones = jnp.ones((512, 128), BF16)

        def weigh(j, _):
            vals = win_ref[pl.ds(pl.multiple_of(j * 512, 512), 512), 256:512]
            for h in range(HEADS):
                w = []
                for i in range(4):
                    s = sbuf[h, :, pl.ds(pl.multiple_of((4 * j + i) * 128, 128), 128)]
                    w.append(jnp.exp2((s - smax[h]) * (LOG2E / ROOT)).astype(BF16))
                v = jnp.concatenate([vals[:, 128 * h : 128 * h + 128], ones], 1)
                acc[h] += jnp.dot(jnp.concatenate(w, 1), v, preferred_element_type=F32)
            return 0

        lax.fori_loop(lo, hi, weigh, 0)

    stats = jnp.zeros((128, 128), F32)
    for h in range(HEADS):
        msg_ref[:, 128 * h : 128 * h + 128] = acc[h, :, 0:128].astype(BF16)
        for n, full in enumerate((smax[h] * (1.0 / ROOT), acc[h, :, 128:256])):
            for part in range(3):
                piece = full.astype(BF16).astype(F32)
                stats = jnp.where(lanes == h * 6 + n * 3 + part, piece, stats)
                full = full - piece
    msg_ref[:, 256:384] = stats.astype(BF16)


def reduce_kernel(pbn, kan, msg_ref, wo_ref, out_ref, slots, send, recv):
    p = lax.axis_index("pb")
    k = lax.axis_index("ka")
    rows = out_ref.shape[0]

    def active(kd):
        b0 = p + 4 * kd - 16
        return (b0 >= -4) & (b0 < pbn)

    barrier = pltpu.get_barrier_semaphore()
    for i in range(1, kan):
        kd = lax.rem(k + i, kan)

        @pl.when(active(kd))
        def _(kd=kd):
            pl.semaphore_signal(barrier, inc=1, device_id=(p, kd), device_id_type=MESH)

    def copy(i):
        kd = lax.rem(k + i, kan)
        return pltpu.make_async_remote_copy(
            src_ref=msg_ref.at[pl.ds(kd * rows, rows)], dst_ref=slots.at[i],
            send_sem=send.at[i], recv_sem=recv.at[i],
            device_id=(p, kd), device_id_type=MESH,
        )

    @pl.when(active(k))
    def _():
        pl.semaphore_wait(barrier, kan - 1)
        for i in range(1, kan):
            copy(i).start()

    own = msg_ref[pl.ds(k * rows, rows), :].astype(F32)
    slots[0] = own.astype(BF16)
    for i in range(1, kan):
        src = lax.rem(k + kan - i, kan)

        @pl.when(active(src))
        def _(i=i):
            copy(i).wait_recv()

        @pl.when(jnp.logical_not(active(src)))
        def _(i=i):
            slots[i] = jnp.zeros(slots.shape[1:], BF16)

    res = []
    for h in range(HEADS):
        tops, tots, nums = [], [], []
        for i in range(kan):
            st = slots[i, :, 256:384].astype(F32)
            live = active(lax.rem(k + kan - i, kan))
            a = 6 * h
            top = st[:, a : a + 1] + st[:, a + 1 : a + 2] + st[:, a + 2 : a + 3]
            tops.append(jnp.where(live, top, NEG))
            tots.append(st[:, a + 3 : a + 4] + st[:, a + 4 : a + 5] + st[:, a + 5 : a + 6])
            nums.append(slots[i, :, 128 * h : 128 * h + 128].astype(F32))
        top = functools.reduce(jnp.maximum, tops)
        num = jnp.zeros((rows, HEAD_DIM), F32)
        tot = jnp.zeros((rows, 1), F32)
        for i in range(kan):
            w = jnp.exp(tops[i] - top)
            num = num + w * nums[i]
            tot = tot + w * tots[i]
        res.append((num / tot).astype(BF16))
    att = jnp.concatenate(res, 1)
    out_ref[...] = jnp.dot(att, wo_ref[...], preferred_element_type=F32).astype(BF16)

    @pl.when(active(k))
    def _():
        for i in range(1, kan):
            copy(i).wait_send()


def shards(pbn, kan, bin_states, contacts, w_query, w_keyval, pair_in, pair_shift, pair_out, w_out):
    vmem = pl.BlockSpec(memory_space=pltpu.VMEM)
    smem = pl.BlockSpec(memory_space=pltpu.SMEM)
    hbm = pl.BlockSpec(memory_space=pl.ANY)
    rows, width = bin_states.shape
    block, offsets = contacts.shape
    hc = HEADS * HEAD_DIM
    window = block + offsets
    q_blk, win = pl.pallas_call(
        functools.partial(gather_kernel, pbn, kan),
        out_shape=(
            jax.ShapeDtypeStruct((block, hc), BF16),
            jax.ShapeDtypeStruct((window, 2 * hc), BF16),
        ),
        in_specs=[vmem, vmem, vmem],
        out_specs=(hbm, hbm),
        scratch_shapes=[
            pltpu.VMEM((rows, hc), BF16),
            pltpu.VMEM((rows, 2 * hc), BF16),
            pltpu.SemaphoreType.DMA((kan,)),
            pltpu.SemaphoreType.DMA,
            pltpu.SemaphoreType.DMA((kan, 3)),
            pltpu.SemaphoreType.DMA((3,)),
            pltpu.SemaphoreType.DMA((2,)),
            pltpu.SemaphoreType.DMA((2,)),
        ],
        compiler_params=pltpu.CompilerParams(collective_id=0, has_side_effects=True),
        name="gather_windows",
    )(bin_states, w_query, w_keyval)

    p = lax.axis_index("pb")
    k = lax.axis_index("ka")
    start = ((p * block + k * offsets - HALF_BAND) // block).astype(jnp.int32).reshape(1)
    tiles = offsets // 128
    rb_count = block // 128
    msg = pl.pallas_call(
        functools.partial(attend_kernel, tiles, pbn),
        grid=(rb_count,),
        out_shape=jax.ShapeDtypeStruct((block, hc + 128), BF16),
        in_specs=[
            smem, smem, smem, smem,
            pl.BlockSpec((128, offsets), lambda r: (r, 0)),
            pl.BlockSpec((128, hc), lambda r: (r, 0)),
            pl.BlockSpec((window, 2 * hc), lambda r: (0, 0), pipeline_mode=pl.Buffered(1)),
        ],
        out_specs=pl.BlockSpec((128, hc + 128), lambda r: (r, 0)),
        scratch_shapes=[
            pltpu.VMEM((HEADS, SEGS, 8, 128), F32),
            pltpu.VMEM((HEADS, 128, (tiles + 8) * 128), F32),
            pltpu.VMEM((HEADS, 128, 128), F32),
            pltpu.VMEM((HEADS, 128, (tiles + 4) * 128), F32),
            pltpu.VMEM((HEADS, 128, 256), F32),
            pltpu.VMEM((tiles, 8, 128), jnp.int32),
            pltpu.VMEM((HEADS, 128, 128), F32),
        ],
        name="attend",
    )(start, pair_in, pair_shift, pair_out, contacts, q_blk, win)

    return pl.pallas_call(
        functools.partial(reduce_kernel, pbn, kan),
        out_shape=jax.ShapeDtypeStruct((rows, width), BF16),
        in_specs=[vmem, vmem],
        out_specs=vmem,
        scratch_shapes=[
            pltpu.VMEM((kan, rows, hc + 128), BF16),
            pltpu.SemaphoreType.DMA((kan,)),
            pltpu.SemaphoreType.DMA((kan,)),
        ],
        compiler_params=pltpu.CompilerParams(collective_id=1, has_side_effects=True),
        name="reduce_rows",
    )(msg, w_out)


def solution(mesh):
    placed = (P(("pb", "ka"), None), P("pb", "ka"), P(), P(), P(), P(), P(), P())
    return jax.shard_map(
        functools.partial(shards, mesh.shape["pb"], mesh.shape["ka"]),
        mesh=mesh, in_specs=placed, out_specs=P(("pb", "ka"), None), check_vma=False,
    )
```

time: 528 us -> 84.7 us (0.16)
  other arithmetic: 248 us -> 0 us
  blocking collectives: 94.4 us -> 0 us
  Pallas kernels: 0 us -> 82.8 us
  waiting for transfers between devices: 70.4 us -> 0 us
  local copies, waits for them, and re-layouts: 69.3 us -> 1.62 us
  matrix products: 20.2 us -> 0 us
  between operations: 13.5 us -> 0.02 us
  starting transfers between devices: 9.46 us -> 0 us
    another operation x3 -> x0, other arithmetic: 234 us -> none  [pair_bias(): return jnp.stack(per_head, 0)]
    pallas_call x0 -> x3, Pallas kernels: none -> 82.8 us  [the longest x1 50.3 us: shards(): pl.pallas_call(functools.partial(reduce_kernel, pbn, kan), out_shape=jax....]
    psum x1 -> x0, waiting for transfers between devices: 68.8 us -> none  [shards(): summed_num, summed_tot = lax.psum((numerators, totals), 'ka')]
    all_gather x2 -> x0, blocking collectives: 60 us -> none  [the longest x1 31.3 us: shards(): lax.all_gather(key_values, 'ka', axis=0, tiled=True)]
    slice x13 -> x0, local copies, waits for them, and re-layouts: 28.1 us -> none  [the longest x1 8.53 us: shear_rows(): flattened = flattened[:, :height * (length + height)]]
    unnamed x28 -> x1, local copies, waits for them, and re-layouts: 22.1 us -> 1.62 us
    dot_general x5 -> x0, matrix products: 20.2 us -> none  [the longest x1 10.8 us: score_block(): jnp.einsum('ihd,khd->hik', rows_query, key_heads, preferred_element_type=...]
    pmax x1 -> x0, blocking collectives: 18.4 us -> none  [shards(): row_top = lax.pmax(jnp.max(scores, axis=3), 'ka')]
  transfers between devices with their start and end apart: 7 -> 0, of which waited for: 2 -> 0; matrix products, arithmetic and copies ran while one was open for 58% -> 0% of each run, Pallas kernels for 0% -> 0%
where the time goes in v1:
time: 84.7 us; the launch traced here: 84.4 us
  Pallas kernels  82.8 us (98%)
  local copies, waits for them, and re-layouts  1.62 us (2%)
    pallas_call x1, Pallas kernels, shards(): pl.pallas_call(functools.partial(reduce_kernel, pbn, kan), out_shape=jax....  50.3 us
    pallas_call x1, Pallas kernels, shards(): pl.pallas_call(functools.partial(gather_kernel, pbn, kan), out_shape=(jax...  27.2 us
    pallas_call x1, Pallas kernels, shards(): pl.pallas_call(functools.partial(attend_kernel, tiles, pbn), grid=(rb_cou...  5.3 us

profile of v1, /device:TPU:16, one launch (start us, length us, event | category | flops | bytes accessed | tf_op | source)
XLA Modules:
  0.0 84.4 jit_solution(14223612428165590678)
XLA Ops:
  0.0 27.2 %gather_windows.1 = (bf16[512,256]{1,0:T(8,128)(2,1)}, bf16[2560,512]{1,0:T(8,128)(2,1)}) custom-call(bf16[64,1536]{1,0:T(8,128)(2,1)} %x_ref.1, bf16[1536,256]{1,0:T(8,128)(2,1)} %wq_ref.1, bf16[1536,512]{1,0:T(8,128)(2,1)} %wkv_ref.1), custom_call_target="tpu_custom_call" | custom-call | tf_op jit(solution)/shard_map/gather_windows/pallas_call | solution.py:406
  27.2 5.3 %attend.1.msg_ref = bf16[512,384]{1,0:T(8,128)(2,1)} custom-call(s32[1]{0:T(128)} %bitcast.start_ref, f32[2,32]{1,0:T(2,128)} %pin_ref.1, f32[2,32]{1,0:T(2,128)} %psh_ref.1, f32[2,32]{1,0:T(2,128)} %pout_ref.1, s32[512,2048]{1,0:T(8,128)} %con_ref.1, bf16[512,256]{1,0:T(8,128)(2,1)} %get-tuple-element.7.q_ref, bf16[2560,512]{1,0:T(8,128)(2,1)} %get-tuple-element.8.win_ref), custom_call_target="tpu_custom_call" | custom-call | tf_op jit(solution)/shard_map/attend/pallas_call | solution.py:433
  32.5 50.3 %reduce_rows.1 = bf16[64,1536]{1,0:T(8,128)(2,1)} custom-call(bf16[512,384]{1,0:T(8,128)(2,1)} %attend.1.msg_ref, bf16[256,1536]{1,0:T(8,128)(2,1)} %wo_ref.1), custom_call_target="tpu_custom_call" | custom-call | tf_op jit(solution)/shard_map/reduce_rows/pallas_call | solution.py:456
  82.8 1.6 %copy.10 = bf16[64,1536]{1,0:T(8,128)(2,1)} copy(bf16[64,1536]{1,0:T(8,128)(2,1)} %reduce_rows.1) | data formatting | bytes 393216

commit v2 on v1

v2 whole, which is shorter than its diff:
```python
import functools
import jax
import jax.numpy as jnp
from jax import lax
from jax.experimental import pallas as pl
from jax.experimental.pallas import tpu as pltpu
from jax.sharding import PartitionSpec as P

HEADS = 2
HEAD_DIM = 128
PAIR_HIDDEN = 32
HALF_BAND = 8192
SEGS = 16
ROOT = HEAD_DIM**0.5
LOG2E = 1.4426950408889634
NEG = -1e30
MESH = pl.DeviceIdType.MESH
F32 = jnp.float32
BF16 = jnp.bfloat16


def pick(table, low):
    dims = lax.GatherDimensionNumbers(
        offset_dims=(), collapsed_slice_dims=(1,), start_index_map=(1,),
        operand_batching_dims=(0,), start_indices_batching_dims=(0,),
    )
    return lax.gather(
        table, low[:, :, None], dims, slice_sizes=(1, 1),
        mode=lax.GatherScatterMode.PROMISE_IN_BOUNDS,
    )


def shear(x):
    return pltpu.roll(x, 0, 1, stride=1, stride_axis=0)


def build_table(pin_ref, psh_ref, pout_ref, tab):
    ids = (
        lax.broadcasted_iota(jnp.int32, (SEGS, 128), 0) * 128
        + lax.broadcasted_iota(jnp.int32, (SEGS, 128), 1)
    )
    logc = jnp.log(1.0 + ids.astype(F32))
    for h in range(HEADS):
        summed = jnp.zeros((SEGS, 128), F32)
        for u in range(PAIR_HIDDEN):
            inner = pin_ref[h, u] * logc + psh_ref[h, u]
            summed = summed + pout_ref[h, u] * (inner / (1.0 + jnp.exp(-inner)))
        summed = summed * ROOT
        for s in range(SEGS):
            tab[h, s] = jnp.broadcast_to(summed[s : s + 1], (8, 128))


def message(rows, tops, sums, msg_ref):
    lanes = lax.broadcasted_iota(jnp.int32, (128, 128), 1)
    stats = jnp.zeros((128, 128), F32)
    for h in range(HEADS):
        msg_ref[rows, 128 * h : 128 * h + 128] = sums[h][:, 0:128].astype(BF16)
        for n, full in enumerate((tops[h] * (1.0 / ROOT), sums[h][:, 128:256])):
            for part in range(3):
                piece = full.astype(BF16).astype(F32)
                stats = jnp.where(lanes == h * 6 + n * 3 + part, piece, stats)
                full = full - piece
    msg_ref[rows, 256:384] = stats.astype(BF16)


def main_kernel(
    pbn, kan, pin_ref, psh_ref, pout_ref, x_hbm, wq_hbm, wkv_hbm, con_hbm,
    msg_ref, odd_ref, q_out, win_out,
    x, wq, wkv, con, qs, kvs, qall, win, tab, bias, sbuf, wbuf, tops, alpha, acc,
    in_sem, con_sem, q_send, q_recv, kv_send, kv_recv, f_send, f_recv, out_sem,
):
    p = lax.axis_index("pb")
    k = lax.axis_index("ka")
    rows = x.shape[0]
    block = rows * kan
    tiles = con.shape[1] // 128
    partner = p + 1 - 2 * (p % 2)
    odd = p % 2
    first = p + 4 * k - 16
    pad = 4
    active = (first >= -4) & (first < pbn)

    loads = [
        pltpu.make_async_copy(x_hbm, x, in_sem.at[0]),
        pltpu.make_async_copy(wkv_hbm, wkv, in_sem.at[1]),
        pltpu.make_async_copy(wq_hbm, wq, in_sem.at[2]),
    ]
    for c in loads:
        c.start()

    def con_load(r):
        at = pl.ds(r * 128, 128)
        return pltpu.make_async_copy(con_hbm.at[at], con.at[at], con_sem.at[r])

    for r in range(4):
        con_load(r).start()

    def dest(kd, m):
        pd = p - 4 * kd + 16 - 2 * m
        return pd, (pd >= 0) & (pd < pbn)

    def has(m):
        b = first + 2 * m
        return (b >= 0) & (b < pbn)

    barrier = pltpu.get_barrier_semaphore()
    for i in range(1, kan):
        pl.semaphore_signal(
            barrier, inc=1, device_id=(p, lax.rem(k + i, kan)), device_id_type=MESH
        )
    pl.semaphore_signal(barrier, inc=1, device_id=(partner, k), device_id_type=MESH)
    for m in range(3):
        b = first + 2 * m
        for i in range(kan):
            own = (b == p) & (i == 0)

            @pl.when(has(m) & jnp.logical_not(own))
            def _(b=b, i=i):
                pl.semaphore_signal(
                    barrier, inc=1, device_id=(b, lax.rem(k + i, kan)), device_id_type=MESH
                )

    expected = kan
    for i in range(kan):
        kd = lax.rem(k + i, kan)
        for m in range(3):
            pd, ok = dest(kd, m)
            own = (pd == p) & (i == 0)
            expected = expected + jnp.where(ok & jnp.logical_not(own), 1, 0)

    loads[0].wait()
    loads[1].wait()
    kvs[...] = jnp.dot(x[...], wkv[...], preferred_element_type=F32).astype(BF16)
    pl.semaphore_wait(barrier, expected)

    def q_copy(i):
        kd = lax.rem(k + i, kan)
        return pltpu.make_async_remote_copy(
            src_ref=qs, dst_ref=qall.at[pl.ds(k * rows, rows)],
            send_sem=q_send.at[i], recv_sem=q_recv,
            device_id=(p, kd), device_id_type=MESH,
        )

    def kv_rows(m):
        return win.at[pl.ds(2 * m * block + k * rows, rows)]

    def kv_copy(i, m, pd, kd):
        return pltpu.make_async_remote_copy(
            src_ref=kvs, dst_ref=kv_rows(m),
            send_sem=kv_send.at[i, m], recv_sem=kv_recv.at[m],
            device_id=(pd, kd), device_id_type=MESH,
        )

    def send_kv(m):
        for i in range(kan):
            kd = lax.rem(k + i, kan)
            pd, ok = dest(kd, m)
            own = (pd == p) & (i == 0)

            @pl.when(ok & jnp.logical_not(own))
            def _(i=i, m=m, pd=pd, kd=kd):
                kv_copy(i, m, pd, kd).start()

            if i == 0:

                @pl.when(ok & own)
                def _(m=m):
                    pltpu.make_async_copy(kvs, kv_rows(m), kv_recv.at[m]).start()

    send_kv(0)
    loads[2].wait()
    qs[...] = jnp.dot(x[...], wq[...], preferred_element_type=F32).astype(BF16)
    for i in range(1, kan):
        q_copy(i).start()
    pltpu.make_async_copy(qs, qall.at[pl.ds(k * rows, rows)], q_recv).start()
    send_kv(1)
    send_kv(2)

    def fwd(slot):
        m = slot + 1 - odd
        return pltpu.make_async_remote_copy(
            src_ref=win.at[pl.ds(2 * m * block, block)],
            dst_ref=win.at[pl.ds((2 * slot + 1) * block, block)],
            send_sem=f_send.at[slot], recv_sem=f_recv.at[slot],
            device_id=(partner, k), device_id_type=MESH,
        )

    def in_block(m):
        part = win.at[pl.ds(2 * m * block, block)]
        return pltpu.make_async_remote_copy(
            src_ref=part, dst_ref=part, send_sem=kv_send.at[0, m], recv_sem=kv_recv.at[m],
            device_id=(partner, k), device_id_type=MESH,
        )

    def keep(j):
        at = pl.ds(j * block, block)
        return pltpu.make_async_copy(win.at[at], win_out.at[at], out_sem.at[j])

    lanes = lax.broadcasted_iota(jnp.int32, (128, 128), 1)
    subl = lax.broadcasted_iota(jnp.int32, (128, 128), 0)
    here = lanes >= subl

    @pl.when(active)
    def _():
        build_table(pin_ref, psh_ref, pout_ref, tab)
        tables = [tab[h, 0] for h in range(HEADS)]
        near = jnp.where(k == 4, 0, jnp.where(k == 3, tiles - 1, -1))
        second = jnp.where(k == 4, 1, jnp.where(k == 3, tiles - 2, -1))

        for r in range(4):
            con_load(r).wait()

        def look_rows(r, every):
            at_r = pl.multiple_of(r * 128, 128)
            band = pl.ds(at_r, 128)
            edge = jnp.full((128, pad * 128), NEG, F32)
            for h in range(HEADS):
                bias[h, band, 0 : pad * 128] = edge
                bias[h, band, (pad + tiles) * 128 : (2 * pad + tiles) * 128] = edge

            def look(it, every):
                for u in range(4):
                    j = it * 4 + u
                    at = pl.multiple_of(j * 128, 128)
                    c = con[band, pl.ds(at, 128)]
                    some = functools.reduce(
                        jnp.bitwise_or, [c[8 * g : 8 * g + 8] for g in range(16)]
                    )
                    beyond = jnp.where(j == near, 0, jnp.where(j == second, -512, -128))
                    every = every | (some & beyond)
                    low = shear(c & 127)
                    for g in range(16):
                        for h in range(HEADS):
                            bias[
                                h, pl.ds(at_r + 8 * g, 8), pl.ds(at + pad * 128, 128)
                            ] = pick(tables[h], low[8 * g : 8 * g + 8])
                return every

            every = lax.fori_loop(0, tiles // 4, look, every)

            def further(j, rounds):
                at = pl.multiple_of(j * 128, 128)
                c = shear(con[band, pl.ds(at, 128)])

                def some_rows(t, _):
                    for g in range(16):
                        low = c[8 * g : 8 * g + 8] & 127
                        row = c[8 * g : 8 * g + 8] >> 7
                        for h in range(HEADS):
                            part = (h, pl.ds(at_r + 8 * g, 8), pl.ds(at + pad * 128, 128))
                            got = bias[part]
                            for u in range(4):
                                got = jnp.where(
                                    row == 4 * t + u, pick(tab[h, 4 * t + u], low), got
                                )
                            bias[part] = got
                    return 0

                lax.fori_loop(0, rounds, some_rows, 0)

            @pl.when(near >= 0)
            def _():
                further(near, SEGS // 4)
                further(second, 1)

            return every

        odd_ref[...] = lax.fori_loop(0, 4, look_rows, jnp.zeros((8, 128), jnp.int32))
        tops[...] = jnp.full(tops.shape, NEG, F32)
        acc[...] = jnp.zeros(acc.shape, F32)

    whole = pltpu.make_async_remote_copy(
        src_ref=qall, dst_ref=qall, send_sem=q_send.at[0], recv_sem=q_recv,
        device_id=(partner, k), device_id_type=MESH,
    )
    whole.wait_recv()
    q_keep = pltpu.make_async_copy(qall, q_out, out_sem.at[5])
    q_keep.start()
    ones = jnp.ones((block, 128), BF16)

    def attend(j):
        at_k = pl.multiple_of(j * block, block)
        for h in range(HEADS):
            keys = win[pl.ds(at_k, block), 128 * h : 128 * h + 128]
            s = jnp.dot(
                qall[:, 128 * h : 128 * h + 128], keys.T, preferred_element_type=F32
            )
            for r in range(4):
                band = slice(128 * r, 128 * r + 128)
                most = None
                for i in range(4):
                    at = pl.multiple_of((pad + 4 * j + i - r) * 128, 128)
                    b = jnp.where(
                        here, bias[h, band, pl.ds(at, 128)], bias[h, band, pl.ds(at - 128, 128)]
                    )
                    part = s[band, 128 * i : 128 * i + 128] + b
                    sbuf[h, band, 128 * i : 128 * i + 128] = part
                    most = part if most is None else jnp.maximum(most, part)
                top = tops[h, band, :]
                new = jnp.maximum(top, jnp.max(most, axis=1, keepdims=True))
                alpha[h, band, :] = jnp.exp2((top - new) * (LOG2E / ROOT))
                tops[h, band, :] = new
                for i in range(4):
                    wbuf[h, band, 128 * i : 128 * i + 128] = jnp.exp2(
                        (sbuf[h, band, 128 * i : 128 * i + 128] - new) * (LOG2E / ROOT)
                    ).astype(BF16)
            vals = win[pl.ds(at_k, block), 256 + 128 * h : 384 + 128 * h]
            new = jnp.dot(
                wbuf[h], jnp.concatenate([vals, ones], 1), preferred_element_type=F32
            )
            a = alpha[h]
            acc[h] = acc[h] * jnp.concatenate([a, a], 1) + new

    def step(it, _):
        j = lax.rem(2 * it, 5)
        b = first + j

        @pl.when((b >= 0) & (b < pbn))
        def _():
            @pl.when(it < 3)
            def _():
                in_block(it).wait_recv()
                slot = it - 1 + odd

                @pl.when((slot >= 0) & (slot < 2))
                def _():
                    fwd(slot).start()

            @pl.when(it >= 3)
            def _():
                fwd(it - 3).wait_recv()

            keep(j).start()
            attend(j)

        return 0

    lax.fori_loop(0, 5, step, 0)

    @pl.when(active)
    def _():
        def finish(r, _):
            band = pl.ds(pl.multiple_of(r * 128, 128), 128)
            message(
                band, [tops[h, band, :] for h in range(HEADS)],
                [acc[h, band, :] for h in range(HEADS)], msg_ref,
            )
            return 0

        lax.fori_loop(0, 4, finish, 0)

    @pl.when(jnp.logical_not(active))
    def _():
        odd_ref[...] = jnp.zeros((8, 128), jnp.int32)
        msg_ref[...] = jnp.zeros(msg_ref.shape, BF16)
        for r in range(4):
            con_load(r).wait()

    def drain(j, _):
        b = first + j

        @pl.when((b >= 0) & (b < pbn))
        def _():
            keep(j).wait()

        return 0

    lax.fori_loop(0, 5, drain, 0)
    q_keep.wait()
    for slot in range(2):
        b_out = first + 2 * (slot + 1 - odd)

        @pl.when((b_out >= 0) & (b_out < pbn))
        def _(slot=slot):
            fwd(slot).wait_send()

    for i in range(kan):
        kd = lax.rem(k + i, kan)
        for m in range(3):
            pd, ok = dest(kd, m)
            own = (pd == p) & (i == 0)

            @pl.when(ok & jnp.logical_not(own))
            def _(i=i, m=m, pd=pd, kd=kd):
                kv_copy(i, m, pd, kd).wait_send()

        if i:
            q_copy(i).wait_send()


def redo_kernel(
    tiles, blocks, start_ref, odd_ref, pin_ref, psh_ref, pout_ref, con_hbm, q_hbm, win_hbm, msg_in,
    msg_out, tab, con, q, win, bias, smax, sbuf, acc, msg, sem,
):
    first = start_ref[0]
    pad = 4

    @pl.when(jnp.max(odd_ref[...].astype(F32)) > 0.5)
    def _():
        lanes = lax.broadcasted_iota(jnp.int32, (128, 128), 1)
        subl = lax.broadcasted_iota(jnp.int32, (128, 128), 0)
        here = lanes >= subl
        build_table(pin_ref, psh_ref, pout_ref, tab)
        lo = jnp.maximum(0, -first)
        hi = jnp.minimum(tiles // 4 + 1, blocks - first)
        edge = jnp.full((128, pad * 128), NEG, F32)
        for h in range(HEADS):
            bias[h, :, 0 : pad * 128] = edge
            bias[h, :, (pad + tiles) * 128 : (2 * pad + tiles) * 128] = edge

        def fetch(src, dst):
            c = pltpu.make_async_copy(src, dst, sem)
            c.start()
            c.wait()

        def load_win(j, _):
            at = pl.ds(pl.multiple_of(j * 512, 512), 512)
            fetch(win_hbm.at[at], win.at[at])
            return 0

        lax.fori_loop(lo, hi, load_win, 0)
        ones = jnp.ones((512, 128), BF16)

        def rows(rb, _):
            band = pl.ds(pl.multiple_of(rb * 128, 128), 128)
            fetch(con_hbm.at[band], con)
            fetch(q_hbm.at[band], q)
            smax[...] = jnp.full(smax.shape, NEG, F32)
            acc[...] = jnp.zeros(acc.shape, F32)

            def look(j, _):
                at = pl.multiple_of(j * 128, 128)
                c = shear(con[:, pl.ds(at, 128)])

                def row(s, _):
                    for g in range(16):
                        part = c[8 * g : 8 * g + 8]
                        for h in range(HEADS):
                            spot = (h, slice(8 * g, 8 * g + 8), pl.ds(at + pad * 128, 128))
                            bias[spot] = jnp.where(
                                (part >> 7) == s, pick(tab[h, s], part & 127), bias[spot]
                            )
                    return 0

                lax.fori_loop(0, SEGS, row, 0)
                return 0

            lax.fori_loop(0, tiles, look, 0)

            def score(j, _):
                for h in range(HEADS):
                    keys = win[
                        pl.ds(pl.multiple_of(j * 512, 512), 512), 128 * h : 128 * h + 128
                    ]
                    s = jnp.dot(
                        q[:, 128 * h : 128 * h + 128], keys.T, preferred_element_type=F32
                    )
                    top = smax[h]
                    for i in range(4):
                        at = pl.multiple_of((pad + 4 * j + i - rb) * 128, 128)
                        b = jnp.where(
                            here, bias[h, :, pl.ds(at, 128)], bias[h, :, pl.ds(at - 128, 128)]
                        )
                        part = s[:, 128 * i : 128 * i + 128] + b
                        sbuf[h, :, pl.ds(pl.multiple_of((4 * j + i) * 128, 128), 128)] = part
                        top = jnp.maximum(top, part)
                    smax[h] = top
                return 0

            lax.fori_loop(lo, hi, score, 0)
            for h in range(HEADS):
                smax[h] = jnp.broadcast_to(jnp.max(smax[h], axis=1, keepdims=True), (128, 128))

            def weigh(j, _):
                for h in range(HEADS):
                    vals = win[
                        pl.ds(pl.multiple_of(j * 512, 512), 512), 256 + 128 * h : 384 + 128 * h
                    ]
                    w = []
                    for i in range(4):
                        s = sbuf[h, :, pl.ds(pl.multiple_of((4 * j + i) * 128, 128), 128)]
                        w.append(jnp.exp2((s - smax[h]) * (LOG2E / ROOT)).astype(BF16))
                    acc[h] += jnp.dot(
                        jnp.concatenate(w, 1), jnp.concatenate([vals, ones], 1),
                        preferred_element_type=F32,
                    )
                return 0

            lax.fori_loop(lo, hi, weigh, 0)
            message(
                slice(0, 128), [smax[h] for h in range(HEADS)],
                [acc[h] for h in range(HEADS)], msg,
            )
            fetch(msg, msg_out.at[band])
            return 0

        lax.fori_loop(0, 4, rows, 0)


def reduce_kernel(pbn, kan, msg_ref, wo_ref, out_ref, slots, send, recv):
    p = lax.axis_index("pb")
    k = lax.axis_index("ka")
    rows = out_ref.shape[0]

    def active(kd):
        b0 = p + 4 * kd - 16
        return (b0 >= -4) & (b0 < pbn)

    barrier = pltpu.get_barrier_semaphore()
    for i in range(1, kan):
        kd = lax.rem(k + i, kan)

        @pl.when(active(kd))
        def _(kd=kd):
            pl.semaphore_signal(barrier, inc=1, device_id=(p, kd), device_id_type=MESH)

    def copy(i):
        kd = lax.rem(k + i, kan)
        return pltpu.make_async_remote_copy(
            src_ref=msg_ref.at[pl.ds(kd * rows, rows)], dst_ref=slots.at[i],
            send_sem=send.at[i], recv_sem=recv.at[i],
            device_id=(p, kd), device_id_type=MESH,
        )

    @pl.when(active(k))
    def _():
        pl.semaphore_wait(barrier, kan - 1)
        for i in range(1, kan):
            copy(i).start()

    own = msg_ref[pl.ds(k * rows, rows), :].astype(F32)
    slots[0] = own.astype(BF16)
    for i in range(1, kan):
        src = lax.rem(k + kan - i, kan)

        @pl.when(active(src))
        def _(i=i):
            copy(i).wait_recv()

        @pl.when(jnp.logical_not(active(src)))
        def _(i=i):
            slots[i] = jnp.zeros(slots.shape[1:], BF16)

    res = []
    for h in range(HEADS):
        tops, tots, nums = [], [], []
        for i in range(kan):
            st = slots[i, :, 256:384].astype(F32)
            live = active(lax.rem(k + kan - i, kan))
            a = 6 * h
            top = st[:, a : a + 1] + st[:, a + 1 : a + 2] + st[:, a + 2 : a + 3]
            tops.append(jnp.where(live, top, NEG))
            tots.append(st[:, a + 3 : a + 4] + st[:, a + 4 : a + 5] + st[:, a + 5 : a + 6])
            nums.append(slots[i, :, 128 * h : 128 * h + 128].astype(F32))
        top = functools.reduce(jnp.maximum, tops)
        num = jnp.zeros((rows, HEAD_DIM), F32)
        tot = jnp.zeros((rows, 1), F32)
        for i in range(kan):
            w = jnp.exp(tops[i] - top)
            num = num + w * nums[i]
            tot = tot + w * tots[i]
        res.append((num / tot).astype(BF16))
    att = jnp.concatenate(res, 1)
    out_ref[...] = jnp.dot(att, wo_ref[...], preferred_element_type=F32).astype(BF16)

    @pl.when(active(k))
    def _():
        for i in range(1, kan):
            copy(i).wait_send()


def shards(pbn, kan, bin_states, contacts, w_query, w_keyval, pair_in, pair_shift, pair_out, w_out):
    vmem = pl.BlockSpec(memory_space=pltpu.VMEM)
    smem = pl.BlockSpec(memory_space=pltpu.SMEM)
    hbm = pl.BlockSpec(memory_space=pl.ANY)
    rows, width = bin_states.shape
    block, offsets = contacts.shape
    hc = HEADS * HEAD_DIM
    window = block + offsets
    tiles = offsets // 128
    msg, odd, q_blk, win = pl.pallas_call(
        functools.partial(main_kernel, pbn, kan),
        out_shape=(
            jax.ShapeDtypeStruct((block, hc + 128), BF16),
            jax.ShapeDtypeStruct((8, 128), jnp.int32),
            jax.ShapeDtypeStruct((block, hc), BF16),
            jax.ShapeDtypeStruct((window, 2 * hc), BF16),
        ),
        in_specs=[smem, smem, smem, hbm, hbm, hbm, hbm],
        out_specs=(vmem, vmem, hbm, hbm),
        scratch_shapes=[
            pltpu.VMEM((rows, width), BF16),
            pltpu.VMEM((width, hc), BF16),
            pltpu.VMEM((width, 2 * hc), BF16),
            pltpu.VMEM((block, offsets), jnp.int32),
            pltpu.VMEM((rows, hc), BF16),
            pltpu.VMEM((rows, 2 * hc), BF16),
            pltpu.VMEM((block, hc), BF16),
            pltpu.VMEM((window, 2 * hc), BF16),
            pltpu.VMEM((HEADS, SEGS, 8, 128), F32),
            pltpu.VMEM((HEADS, block, (tiles + 8) * 128), F32),
            pltpu.VMEM((HEADS, block, block), F32),
            pltpu.VMEM((HEADS, block, block), BF16),
            pltpu.VMEM((HEADS, block, 128), F32),
            pltpu.VMEM((HEADS, block, 128), F32),
            pltpu.VMEM((HEADS, block, 256), F32),
            pltpu.SemaphoreType.DMA((3,)),
            pltpu.SemaphoreType.DMA((4,)),
            pltpu.SemaphoreType.DMA((kan,)),
            pltpu.SemaphoreType.DMA,
            pltpu.SemaphoreType.DMA((kan, 3)),
            pltpu.SemaphoreType.DMA((3,)),
            pltpu.SemaphoreType.DMA((2,)),
            pltpu.SemaphoreType.DMA((2,)),
            pltpu.SemaphoreType.DMA((6,)),
        ],
        compiler_params=pltpu.CompilerParams(collective_id=0, has_side_effects=True),
        name="gather_attend",
    )(pair_in, pair_shift, pair_out, bin_states, w_query, w_keyval, contacts)

    p = lax.axis_index("pb")
    k = lax.axis_index("ka")
    start = ((p * block + k * offsets - HALF_BAND) // block).astype(jnp.int32).reshape(1)
    msg = pl.pallas_call(
        functools.partial(redo_kernel, tiles, pbn),
        out_shape=jax.ShapeDtypeStruct((block, hc + 128), BF16),
        in_specs=[smem, vmem, smem, smem, smem, hbm, hbm, hbm, hbm],
        out_specs=hbm,
        scratch_shapes=[
            pltpu.VMEM((HEADS, SEGS, 8, 128), F32),
            pltpu.VMEM((128, offsets), jnp.int32),
            pltpu.VMEM((128, hc), BF16),
            pltpu.VMEM((window, 2 * hc), BF16),
            pltpu.VMEM((HEADS, 128, (tiles + 8) * 128), F32),
            pltpu.VMEM((HEADS, 128, 128), F32),
            pltpu.VMEM((HEADS, 128, (tiles + 4) * 128), F32),
            pltpu.VMEM((HEADS, 128, 256), F32),
            pltpu.VMEM((128, hc + 128), BF16),
            pltpu.SemaphoreType.DMA,
        ],
        input_output_aliases={8: 0},
        name="redo",
    )(start, odd, pair_in, pair_shift, pair_out, contacts, q_blk, win, msg)

    return pl.pallas_call(
        functools.partial(reduce_kernel, pbn, kan),
        out_shape=jax.ShapeDtypeStruct((rows, width), BF16),
        in_specs=[vmem, vmem],
        out_specs=vmem,
        scratch_shapes=[
            pltpu.VMEM((kan, rows, hc + 128), BF16),
            pltpu.SemaphoreType.DMA((kan,)),
            pltpu.SemaphoreType.DMA((kan,)),
        ],
        compiler_params=pltpu.CompilerParams(collective_id=1, has_side_effects=True),
        name="reduce_rows",
    )(msg, w_out)


def solution(mesh):
    placed = (P(("pb", "ka"), None), P("pb", "ka"), P(), P(), P(), P(), P(), P())
    return jax.shard_map(
        functools.partial(shards, mesh.shape["pb"], mesh.shape["ka"]),
        mesh=mesh, in_specs=placed, out_specs=P(("pb", "ka"), None), check_vma=False,
    )
```

time: 84.7 us -> 52.5 us (0.62)
  Pallas kernels: 82.8 us -> 50.3 us
    pallas_call x1, Pallas kernels: 50.3 us -> 22.3 us  [shards(): pl.pallas_call(functools.partial(reduce_kernel, pbn, kan), out_shape=jax....]
    pallas_call x2, Pallas kernels: 32.5 us -> 27.9 us  [the longest x1 27 us: shards(): pl.pallas_call(functools.partial(main_kernel, pbn, kan), out_shape=(jax.S...]
where the time goes in v2:
time: 52.5 us; the launch traced here: 51.9 us
  Pallas kernels  50.3 us (96%)
  local copies, waits for them, and re-layouts  1.62 us (3%)
    pallas_call x1, Pallas kernels, shards(): pl.pallas_call(functools.partial(main_kernel, pbn, kan), out_shape=(jax.S...  27 us
    pallas_call x1, Pallas kernels, shards(): pl.pallas_call(functools.partial(reduce_kernel, pbn, kan), out_shape=jax....  22.3 us
    unnamed x1, local copies, waits for them, and re-layouts  1.62 us

profile of v2, /device:TPU:16, one launch (start us, length us, event | category | flops | bytes accessed | tf_op | source)
XLA Modules:
  0.0 51.9 jit_solution(11692537811466589463)
XLA Ops:
  0.0 27.0 %gather_attend.1 = (bf16[512,384]{1,0:T(8,128)(2,1)}, s32[8,128]{1,0:T(8,128)}, bf16[512,256]{1,0:T(8,128)(2,1)}, bf16[2560,512]{1,0:T(8,128)(2,1)}) custom-call(f32[2,32]{1,0:T(2,128)} %pin_ref.3, f32[2,32]{1,0:T(2,128)} %psh_ref.3, f32[2,32]{1,0:T(2,128)} %pout_ref.3, bf16[64,1536]{1,0:T(8,128)(2,1)} %x_hbm.1, bf16[1536,256]{1,0:T(8,128)(2,1)} %wq_hbm.1, ...), custom_call_target="tpu_custom_call" | custom-call | tf_op jit(solution)/shard_map/gather_attend/pallas_call | solution.py:581
  27.0 1.0 %redo.1.msg_ref = bf16[512,384]{1,0:T(8,128)(2,1)} custom-call(s32[1]{0:T(128)} %bitcast.start_ref, s32[8,128]{1,0:T(8,128)} %get-tuple-element.9.odd_ref, f32[2,32]{1,0:T(2,128)} %pin_ref.3, f32[2,32]{1,0:T(2,128)} %psh_ref.3, f32[2,32]{1,0:T(2,128)} %pout_ref.3, s32[512,2048]{1,0:T(8,128)} %con_hbm.3, ...), custom_call_target="tpu_custom_call", output_to_operand_aliasing={{}: (8, {})} | custom-call | tf_op jit(solution)/shard_map/redo/pallas_call | solution.py:624
  28.0 22.3 %reduce_rows.1 = bf16[64,1536]{1,0:T(8,128)(2,1)} custom-call(bf16[512,384]{1,0:T(8,128)(2,1)} %redo.1.msg_ref, bf16[256,1536]{1,0:T(8,128)(2,1)} %wo_ref.1), custom_call_target="tpu_custom_call" | custom-call | tf_op jit(solution)/shard_map/reduce_rows/pallas_call | solution.py:645
  50.3 1.6 %copy.12 = bf16[64,1536]{1,0:T(8,128)(2,1)} copy(bf16[64,1536]{1,0:T(8,128)(2,1)} %reduce_rows.1) | data formatting | bytes 393216

commit v3 on v2

--- a/solution.py
+++ b/solution.py
@@ -50,22 +50,22 @@
             tab[h, s] = jnp.broadcast_to(summed[s : s + 1], (8, 128))
 
 
-def message(rows, tops, sums, msg_ref):
+def message(rows, tops, sums, num_ref, stat_ref):
     lanes = lax.broadcasted_iota(jnp.int32, (128, 128), 1)
     stats = jnp.zeros((128, 128), F32)
     for h in range(HEADS):
-        msg_ref[rows, 128 * h : 128 * h + 128] = sums[h][:, 0:128].astype(BF16)
+        num_ref[rows, 128 * h : 128 * h + 128] = sums[h][:, 0:128].astype(BF16)
         for n, full in enumerate((tops[h] * (1.0 / ROOT), sums[h][:, 128:256])):
             for part in range(3):
                 piece = full.astype(BF16).astype(F32)
                 stats = jnp.where(lanes == h * 6 + n * 3 + part, piece, stats)
                 full = full - piece
-    msg_ref[rows, 256:384] = stats.astype(BF16)
+    stat_ref[...] = stats.T[0:16, :].astype(BF16)
 
 
 def main_kernel(
     pbn, kan, pin_ref, psh_ref, pout_ref, x_hbm, wq_hbm, wkv_hbm, con_hbm,
-    msg_ref, odd_ref, q_out, win_out,
+    num_ref, stat_ref, odd_ref, q_out, win_out,
     x, wq, wkv, con, qs, kvs, qall, win, tab, bias, sbuf, wbuf, tops, alpha, acc,
     in_sem, con_sem, q_send, q_recv, kv_send, kv_recv, f_send, f_recv, out_sem,
 ):
@@ -92,9 +92,6 @@
         at = pl.ds(r * 128, 128)
         return pltpu.make_async_copy(con_hbm.at[at], con.at[at], con_sem.at[r])
 
-    for r in range(4):
-        con_load(r).start()
-
     def dest(kd, m):
         pd = p - 4 * kd + 16 - 2 * m
         return pd, (pd >= 0) & (pd < pbn)
@@ -128,8 +125,20 @@
             own = (pd == p) & (i == 0)
             expected = expected + jnp.where(ok & jnp.logical_not(own), 1, 0)
 
+    @pl.when(active)
+    def _():
+        build_table(pin_ref, psh_ref, pout_ref, tab)
+        edge = jnp.full((block, (pad + 1) * 128), NEG, F32)
+        for h in range(HEADS):
+            bias[h, :, 0 : (pad + 1) * 128] = edge
+            bias[h, :, (pad + tiles) * 128 : (2 * pad + tiles) * 128] = edge[:, 128:]
+        tops[...] = jnp.full(tops.shape, NEG, F32)
+        acc[...] = jnp.zeros(acc.shape, F32)
+
     loads[0].wait()
     loads[1].wait()
+    for r in range(4):
+        con_load(r).start()
     kvs[...] = jnp.dot(x[...], wkv[...], preferred_element_type=F32).astype(BF16)
     pl.semaphore_wait(barrier, expected)
 
@@ -170,9 +179,20 @@
     send_kv(0)
     loads[2].wait()
     qs[...] = jnp.dot(x[...], wq[...], preferred_element_type=F32).astype(BF16)
+    def wanted(i):
+        b0 = p + 4 * lax.rem(k + i, kan) - 16
+        return (b0 >= -4) & (b0 < pbn)
+
     for i in range(1, kan):
-        q_copy(i).start()
-    pltpu.make_async_copy(qs, qall.at[pl.ds(k * rows, rows)], q_recv).start()
+
+        @pl.when(wanted(i))
+        def _(i=i):
+            q_copy(i).start()
+
+    @pl.when(active)
+    def _():
+        pltpu.make_async_copy(qs, qall.at[pl.ds(k * rows, rows)], q_recv).start()
+
     send_kv(1)
     send_kv(2)
 
@@ -202,7 +222,6 @@
 
     @pl.when(active)
     def _():
-        build_table(pin_ref, psh_ref, pout_ref, tab)
         tables = [tab[h, 0] for h in range(HEADS)]
         near = jnp.where(k == 4, 0, jnp.where(k == 3, tiles - 1, -1))
         second = jnp.where(k == 4, 1, jnp.where(k == 3, tiles - 2, -1))
@@ -210,14 +229,16 @@
         for r in range(4):
             con_load(r).wait()
 
+        def put(h, row, at, g, val):
+            where = pl.ds(row, 8)
+            mask = here[8 * g : 8 * g + 8]
+            at = at + pad * 128
+            pltpu.store(bias.at[h, where, pl.ds(at, 128)], val, mask=mask)
+            pltpu.store(bias.at[h, where, pl.ds(at + 128, 128)], val, mask=jnp.logical_not(mask))
+
         def look_rows(r, every):
             at_r = pl.multiple_of(r * 128, 128)
             band = pl.ds(at_r, 128)
-            edge = jnp.full((128, pad * 128), NEG, F32)
-            for h in range(HEADS):
-                bias[h, band, 0 : pad * 128] = edge
-                bias[h, band, (pad + tiles) * 128 : (2 * pad + tiles) * 128] = edge
-
             def look(it, every):
                 for u in range(4):
                     j = it * 4 + u
@@ -231,54 +252,48 @@
                     low = shear(c & 127)
                     for g in range(16):
                         for h in range(HEADS):
-                            bias[
-                                h, pl.ds(at_r + 8 * g, 8), pl.ds(at + pad * 128, 128)
-                            ] = pick(tables[h], low[8 * g : 8 * g + 8])
+                            put(h, at_r + 8 * g, at, g, pick(tables[h], low[8 * g : 8 * g + 8]))
                 return every
 
             every = lax.fori_loop(0, tiles // 4, look, every)
 
-            def further(j, rounds):
+            def further(j, count):
                 at = pl.multiple_of(j * 128, 128)
                 c = shear(con[band, pl.ds(at, 128)])
-
-                def some_rows(t, _):
-                    for g in range(16):
-                        low = c[8 * g : 8 * g + 8] & 127
-                        row = c[8 * g : 8 * g + 8] >> 7
+                for g in range(16):
+                    low = c[8 * g : 8 * g + 8] & 127
+                    row = c[8 * g : 8 * g + 8] >> 7
+                    got = [pick(tables[h], low) for h in range(HEADS)]
+                    for u in range(1, count):
+                        hit = row == u
                         for h in range(HEADS):
-                            part = (h, pl.ds(at_r + 8 * g, 8), pl.ds(at + pad * 128, 128))
-                            got = bias[part]
-                            for u in range(4):
-                                got = jnp.where(
-                                    row == 4 * t + u, pick(tab[h, 4 * t + u], low), got
-                                )
-                            bias[part] = got
-                    return 0
-
-                lax.fori_loop(0, rounds, some_rows, 0)
+                            got[h] = jnp.where(hit, pick(tab[h, u], low), got[h])
+                    for h in range(HEADS):
+                        put(h, at_r + 8 * g, at, g, got[h])
 
             @pl.when(near >= 0)
             def _():
-                further(near, SEGS // 4)
-                further(second, 1)
+                further(near, SEGS)
+                further(second, 4)
 
             return every
 
         odd_ref[...] = lax.fori_loop(0, 4, look_rows, jnp.zeros((8, 128), jnp.int32))
-        tops[...] = jnp.full(tops.shape, NEG, F32)
-        acc[...] = jnp.zeros(acc.shape, F32)
 
     whole = pltpu.make_async_remote_copy(
         src_ref=qall, dst_ref=qall, send_sem=q_send.at[0], recv_sem=q_recv,
         device_id=(partner, k), device_id_type=MESH,
     )
-    whole.wait_recv()
     q_keep = pltpu.make_async_copy(qall, q_out, out_sem.at[5])
-    q_keep.start()
+
+    @pl.when(active)
+    def _():
+        whole.wait_recv()
+        q_keep.start()
+
     ones = jnp.ones((block, 128), BF16)
 
-    def attend(j):
+    def attend(j, outside):
         at_k = pl.multiple_of(j * block, block)
         for h in range(HEADS):
             keys = win[pl.ds(at_k, block), 128 * h : 128 * h + 128]
@@ -287,13 +302,11 @@
             )
             for r in range(4):
                 band = slice(128 * r, 128 * r + 128)
+                used = [i for i in range(4) if not outside(i, r)]
                 most = None
-                for i in range(4):
+                for i in used:
                     at = pl.multiple_of((pad + 4 * j + i - r) * 128, 128)
-                    b = jnp.where(
-                        here, bias[h, band, pl.ds(at, 128)], bias[h, band, pl.ds(at - 128, 128)]
-                    )
-                    part = s[band, 128 * i : 128 * i + 128] + b
+                    part = s[band, 128 * i : 128 * i + 128] + bias[h, band, pl.ds(at, 128)]
                     sbuf[h, band, 128 * i : 128 * i + 128] = part
                     most = part if most is None else jnp.maximum(most, part)
                 top = tops[h, band, :]
@@ -301,9 +314,11 @@
                 alpha[h, band, :] = jnp.exp2((top - new) * (LOG2E / ROOT))
                 tops[h, band, :] = new
                 for i in range(4):
-                    wbuf[h, band, 128 * i : 128 * i + 128] = jnp.exp2(
-                        (sbuf[h, band, 128 * i : 128 * i + 128] - new) * (LOG2E / ROOT)
-                    ).astype(BF16)
+                    spot = (h, band, slice(128 * i, 128 * i + 128))
+                    if i in used:
+                        wbuf[spot] = jnp.exp2((sbuf[spot] - new) * (LOG2E / ROOT)).astype(BF16)
+                    else:
+                        wbuf[spot] = jnp.zeros((128, 128), BF16)
             vals = win[pl.ds(at_k, block), 256 + 128 * h : 384 + 128 * h]
             new = jnp.dot(
                 wbuf[h], jnp.concatenate([vals, ones], 1), preferred_element_type=F32
@@ -331,7 +346,18 @@
                 fwd(it - 3).wait_recv()
 
             keep(j).start()
-            attend(j)
+
+            @pl.when(j == 0)
+            def _():
+                attend(j, lambda i, r: i < r)
+
+            @pl.when(j == 4)
+            def _():
+                attend(j, lambda i, r: i > r)
+
+            @pl.when((j > 0) & (j < 4))
+            def _():
+                attend(j, lambda i, r: False)
 
         return 0
 
@@ -343,7 +369,7 @@
             band = pl.ds(pl.multiple_of(r * 128, 128), 128)
             message(
                 band, [tops[h, band, :] for h in range(HEADS)],
-                [acc[h, band, :] for h in range(HEADS)], msg_ref,
+                [acc[h, band, :] for h in range(HEADS)], num_ref, stat_ref.at[r],
             )
             return 0
 
@@ -352,7 +378,8 @@
     @pl.when(jnp.logical_not(active))
     def _():
         odd_ref[...] = jnp.zeros((8, 128), jnp.int32)
-        msg_ref[...] = jnp.zeros(msg_ref.shape, BF16)
+        num_ref[...] = jnp.zeros(num_ref.shape, BF16)
+        stat_ref[...] = jnp.zeros(stat_ref.shape, BF16)
         for r in range(4):
             con_load(r).wait()
 
@@ -366,7 +393,11 @@
         return 0
 
     lax.fori_loop(0, 5, drain, 0)
-    q_keep.wait()
+
+    @pl.when(active)
+    def _():
+        q_keep.wait()
+
     for slot in range(2):
         b_out = first + 2 * (slot + 1 - odd)
 
@@ -385,12 +416,15 @@
                 kv_copy(i, m, pd, kd).wait_send()
 
         if i:
-            q_copy(i).wait_send()
+
+            @pl.when(wanted(i))
+            def _(i=i):
+                q_copy(i).wait_send()
 
 
 def redo_kernel(
-    tiles, blocks, start_ref, odd_ref, pin_ref, psh_ref, pout_ref, con_hbm, q_hbm, win_hbm, msg_in,
-    msg_out, tab, con, q, win, bias, smax, sbuf, acc, msg, sem,
+    tiles, blocks, start_ref, odd_ref, pin_ref, psh_ref, pout_ref, con_hbm, q_hbm, win_hbm, num_in,
+    stat_in, num_out, stat_out, tab, con, q, win, bias, smax, sbuf, acc, num, stat, sem,
 ):
     first = start_ref[0]
     pad = 4
@@ -489,15 +523,16 @@
             lax.fori_loop(lo, hi, weigh, 0)
             message(
                 slice(0, 128), [smax[h] for h in range(HEADS)],
-                [acc[h] for h in range(HEADS)], msg,
+                [acc[h] for h in range(HEADS)], num, stat,
             )
-            fetch(msg, msg_out.at[band])
+            fetch(num, num_out.at[band])
+            fetch(stat, stat_out.at[rb])
             return 0
 
         lax.fori_loop(0, 4, rows, 0)
 
 
-def reduce_kernel(pbn, kan, msg_ref, wo_ref, out_ref, slots, send, recv):
+def reduce_kernel(pbn, kan, num_ref, stat_ref, out_ref, nums, stats, send, recv, st_send, st_recv):
     p = lax.axis_index("pb")
     k = lax.axis_index("ka")
     rows = out_ref.shape[0]
@@ -514,59 +549,76 @@
         def _(kd=kd):
             pl.semaphore_signal(barrier, inc=1, device_id=(p, kd), device_id_type=MESH)
 
-    def copy(i):
+    def copies(i):
         kd = lax.rem(k + i, kan)
-        return pltpu.make_async_remote_copy(
-            src_ref=msg_ref.at[pl.ds(kd * rows, rows)], dst_ref=slots.at[i],
-            send_sem=send.at[i], recv_sem=recv.at[i],
-            device_id=(p, kd), device_id_type=MESH,
+        to = {"device_id": (p, kd), "device_id_type": MESH}
+        return (
+            pltpu.make_async_remote_copy(
+                src_ref=stat_ref.at[kd // 2], dst_ref=stats.at[i],
+                send_sem=st_send.at[i], recv_sem=st_recv.at[i], **to,
+            ),
+            pltpu.make_async_remote_copy(
+                src_ref=num_ref.at[pl.ds(kd * rows, rows)], dst_ref=nums.at[i],
+                send_sem=send.at[i], recv_sem=recv.at[i], **to,
+            ),
         )
 
     @pl.when(active(k))
     def _():
         pl.semaphore_wait(barrier, kan - 1)
         for i in range(1, kan):
-            copy(i).start()
-
-    own = msg_ref[pl.ds(k * rows, rows), :].astype(F32)
-    slots[0] = own.astype(BF16)
+            for c in copies(i):
+                c.start()
+
+    nums[0] = num_ref[pl.ds(pl.multiple_of(k * rows, rows), rows), :]
+    stats[0] = stat_ref[k // 2]
     for i in range(1, kan):
         src = lax.rem(k + kan - i, kan)
 
         @pl.when(active(src))
         def _(i=i):
-            copy(i).wait_recv()
+            copies(i)[0].wait_recv()
 
         @pl.when(jnp.logical_not(active(src)))
         def _(i=i):
-            slots[i] = jnp.zeros(slots.shape[1:], BF16)
-
-    res = []
+            nums[i] = jnp.zeros(nums.shape[1:], BF16)
+            stats[i] = jnp.zeros(stats.shape[1:], BF16)
+
+    shares = []
     for h in range(HEADS):
-        tops, tots, nums = [], [], []
+        tops, tots = [], []
         for i in range(kan):
-            st = slots[i, :, 256:384].astype(F32)
+            st = stats[i].astype(F32)
             live = active(lax.rem(k + kan - i, kan))
             a = 6 * h
-            top = st[:, a : a + 1] + st[:, a + 1 : a + 2] + st[:, a + 2 : a + 3]
+            top = st[a : a + 1] + st[a + 1 : a + 2] + st[a + 2 : a + 3]
             tops.append(jnp.where(live, top, NEG))
-            tots.append(st[:, a + 3 : a + 4] + st[:, a + 4 : a + 5] + st[:, a + 5 : a + 6])
-            nums.append(slots[i, :, 128 * h : 128 * h + 128].astype(F32))
+            tots.append(st[a + 3 : a + 4] + st[a + 4 : a + 5] + st[a + 5 : a + 6])
         top = functools.reduce(jnp.maximum, tops)
+        w = [jnp.exp(t - top) for t in tops]
+        tot = functools.reduce(jnp.add, [a * b for a, b in zip(w, tots)])
+        shares += [a / tot for a in w]
+    cols = jnp.concatenate(shares + [jnp.zeros((128 - len(shares), 128), F32)], 0).T
+    cols = jnp.where(lax.rem(k, 2) == 0, cols[0:rows], cols[rows : 2 * rows])
+
+    for i in range(1, kan):
+
+        @pl.when(active(lax.rem(k + kan - i, kan)))
+        def _(i=i):
+            copies(i)[1].wait_recv()
+
+    for h in range(HEADS):
         num = jnp.zeros((rows, HEAD_DIM), F32)
-        tot = jnp.zeros((rows, 1), F32)
         for i in range(kan):
-            w = jnp.exp(tops[i] - top)
-            num = num + w * nums[i]
-            tot = tot + w * tots[i]
-        res.append((num / tot).astype(BF16))
-    att = jnp.concatenate(res, 1)
-    out_ref[...] = jnp.dot(att, wo_ref[...], preferred_element_type=F32).astype(BF16)
+            at = kan * h + i
+            num = num + cols[:, at : at + 1] * nums[i, :, 128 * h : 128 * h + 128].astype(F32)
+        out_ref[:, 128 * h : 128 * h + 128] = num.astype(BF16)
 
     @pl.when(active(k))
     def _():
         for i in range(1, kan):
-            copy(i).wait_send()
+            for c in copies(i):
+                c.wait_send()
 
 
 def shards(pbn, kan, bin_states, contacts, w_query, w_keyval, pair_in, pair_shift, pair_out, w_out):
@@ -578,16 +630,17 @@
     hc = HEADS * HEAD_DIM
     window = block + offsets
     tiles = offsets // 128
-    msg, odd, q_blk, win = pl.pallas_call(
+    num, stat, odd, q_blk, win = pl.pallas_call(
         functools.partial(main_kernel, pbn, kan),
         out_shape=(
-            jax.ShapeDtypeStruct((block, hc + 128), BF16),
+            jax.ShapeDtypeStruct((block, hc), BF16),
+            jax.ShapeDtypeStruct((block // 128, 16, 128), BF16),
             jax.ShapeDtypeStruct((8, 128), jnp.int32),
             jax.ShapeDtypeStruct((block, hc), BF16),
             jax.ShapeDtypeStruct((window, 2 * hc), BF16),
         ),
         in_specs=[smem, smem, smem, hbm, hbm, hbm, hbm],
-        out_specs=(vmem, vmem, hbm, hbm),
+        out_specs=(vmem, vmem, vmem, hbm, hbm),
         scratch_shapes=[
             pltpu.VMEM((rows, width), BF16),
             pltpu.VMEM((width, hc), BF16),
@@ -621,11 +674,14 @@
     p = lax.axis_index("pb")
     k = lax.axis_index("ka")
     start = ((p * block + k * offsets - HALF_BAND) // block).astype(jnp.int32).reshape(1)
-    msg = pl.pallas_call(
+    num, stat = pl.pallas_call(
         functools.partial(redo_kernel, tiles, pbn),
-        out_shape=jax.ShapeDtypeStruct((block, hc + 128), BF16),
-        in_specs=[smem, vmem, smem, smem, smem, hbm, hbm, hbm, hbm],
-        out_specs=hbm,
+        out_shape=(
+            jax.ShapeDtypeStruct((block, hc), BF16),
+            jax.ShapeDtypeStruct((block // 128, 16, 128), BF16),
+        ),
+        in_specs=[smem, vmem, smem, smem, smem, hbm, hbm, hbm, hbm, hbm],
+        out_specs=(hbm, hbm),
         scratch_shapes=[
             pltpu.VMEM((HEADS, SEGS, 8, 128), F32),
             pltpu.VMEM((128, offsets), jnp.int32),
@@ -635,26 +691,31 @@
             pltpu.VMEM((HEADS, 128, 128), F32),
             pltpu.VMEM((HEADS, 128, (tiles + 4) * 128), F32),
             pltpu.VMEM((HEADS, 128, 256), F32),
-            pltpu.VMEM((128, hc + 128), BF16),
+            pltpu.VMEM((128, hc), BF16),
+            pltpu.VMEM((16, 128), BF16),
             pltpu.SemaphoreType.DMA,
         ],
-        input_output_aliases={8: 0},
+        input_output_aliases={8: 0, 9: 1},
         name="redo",
-    )(start, odd, pair_in, pair_shift, pair_out, contacts, q_blk, win, msg)
-
-    return pl.pallas_call(
+    )(start, odd, pair_in, pair_shift, pair_out, contacts, q_blk, win, num, stat)
+
+    att = pl.pallas_call(
         functools.partial(reduce_kernel, pbn, kan),
-        out_shape=jax.ShapeDtypeStruct((rows, width), BF16),
+        out_shape=jax.ShapeDtypeStruct((rows, hc), BF16),
         in_specs=[vmem, vmem],
         out_specs=vmem,
         scratch_shapes=[
-            pltpu.VMEM((kan, rows, hc + 128), BF16),
+            pltpu.VMEM((kan, rows, hc), BF16),
+            pltpu.VMEM((kan, 16, 128), BF16),
+            pltpu.SemaphoreType.DMA((kan,)),
+            pltpu.SemaphoreType.DMA((kan,)),
             pltpu.SemaphoreType.DMA((kan,)),
             pltpu.SemaphoreType.DMA((kan,)),
         ],
         compiler_params=pltpu.CompilerParams(collective_id=1, has_side_effects=True),
         name="reduce_rows",
-    )(msg, w_out)
+    )(num, stat)
+    return jnp.dot(att, w_out, preferred_element_type=F32).astype(BF16)
 
 
 def solution(mesh):

time: 52.5 us -> 49.2 us (0.937)
  the two profiles are of different devices: /device:TPU:16 before, /device:TPU:26 now
where the time goes in v3:
time: 49.2 us; the launch traced here: 48.9 us
  Pallas kernels  47.2 us (96%)
  matrix products  1.69 us (3%)
    pallas_call x1, Pallas kernels, shards(): pl.pallas_call(functools.partial(main_kernel, pbn, kan), out_shape=(jax.S...  36.3 us
    pallas_call x1, Pallas kernels, shards(): pl.pallas_call(functools.partial(reduce_kernel, pbn, kan), out_shape=jax....  9.95 us
    dot_general x1, matrix products, shards(): return jnp.dot(att, w_out, preferred_element_type=F32).astype(BF16)  1.69 us
    pallas_call x1, Pallas kernels, shards(): pl.pallas_call(functools.partial(redo_kernel, tiles, pbn), out_shape=(jax...  0.99 us

profile of v3, /device:TPU:26, one launch (start us, length us, event | category | flops | bytes accessed | tf_op | source)
XLA Modules:
  0.0 48.9 jit_solution(13125889410763011436)
XLA Ops:
  0.0 0.0 copy-start
  0.0 36.3 %gather_attend.1 = (bf16[512,256]{1,0:T(8,128)(2,1)}, bf16[4,16,128]{2,1,0:T(8,128)(2,1)}, s32[8,128]{1,0:T(8,128)}, bf16[512,256]{1,0:T(8,128)(2,1)}, bf16[2560,512]{1,0:T(8,128)(2,1)}) custom-call(f32[2,32]{1,0:T(2,128)} %pin_ref.3, f32[2,32]{1,0:T(2,128)} %psh_ref.3, f32[2,32]{1,0:T(2,128)} %pout_ref.3, bf16[64,1536]{1,0:T(8,128)(2,1)} %x_hbm.1, ...), custom_call_target="tpu_custom_call" | custom-call | tf_op jit(solution)/shard_map/gather_attend/pallas_call | solution.py:633
  36.3 1.0 %redo.1 = (bf16[512,256]{1,0:T(8,128)(2,1)}, bf16[4,16,128]{2,1,0:T(8,128)(2,1)}) custom-call(s32[1]{0:T(128)} %bitcast.start_ref, s32[8,128]{1,0:T(8,128)} %get-tuple-element.12.odd_ref, f32[2,32]{1,0:T(2,128)} %pin_ref.3, f32[2,32]{1,0:T(2,128)} %psh_ref.3, f32[2,32]{1,0:T(2,128)} %pout_ref.3, ...), custom_call_target="tpu_custom_call", output_to_operand_aliasing={{0}: (8, {}), {1}: (9, {})} | custom-call | tf_op jit(solution)/shard_map/redo/pallas_call | solution.py:677
  37.3 9.9 %reduce_rows.1 = bf16[64,256]{1,0:T(8,128)(2,1)} custom-call(bf16[512,256]{1,0:T(8,128)(2,1)} %get-tuple-element.17.num_ref, bf16[4,16,128]{2,1,0:T(8,128)(2,1)} %get-tuple-element.18.stat_ref), custom_call_target="tpu_custom_call" | custom-call | tf_op jit(solution)/shard_map/reduce_rows/pallas_call | solution.py:702
  47.2 0.0 copy-done
  47.2 1.7 %convolution_convert_fusion = bf16[64,1536]{1,0:T(8,128)(2,1)} fusion(bf16[64,256]{1,0:T(8,128)(2,1)} %reduce_rows.1, bf16[256,1536]{1,0:T(8,128)(2,1)S(1)} %copy-done), kind=kOutput, calls=%fused_computation | convolution fusion | flops 50429952 | bytes 1015808 | tf_op jit(solution)/shard_map/dot_general | solution.py:718
Async XLA Ops:
  0.0 47.2 %copy-start = (bf16[256,1536]{1,0:T(8,128)(2,1)S(1)}, bf16[256,1536]{1,0:T(8,128)(2,1)}, u32[]{:S(2)}) copy-start(bf16[256,1536]{1,0:T(8,128)(2,1)} %param.15) | copy-start | bytes 2359300

commit v4 on v3

--- a/solution.py
+++ b/solution.py
@@ -140,6 +140,8 @@
     for r in range(4):
         con_load(r).start()
     kvs[...] = jnp.dot(x[...], wkv[...], preferred_element_type=F32).astype(BF16)
+    loads[2].wait()
+    qs[...] = jnp.dot(x[...], wq[...], preferred_element_type=F32).astype(BF16)
     pl.semaphore_wait(barrier, expected)
 
     def q_copy(i):
@@ -176,9 +178,6 @@
                 def _(m=m):
                     pltpu.make_async_copy(kvs, kv_rows(m), kv_recv.at[m]).start()
 
-    send_kv(0)
-    loads[2].wait()
-    qs[...] = jnp.dot(x[...], wq[...], preferred_element_type=F32).astype(BF16)
     def wanted(i):
         b0 = p + 4 * lax.rem(k + i, kan) - 16
         return (b0 >= -4) & (b0 < pbn)
@@ -193,6 +192,7 @@
     def _():
         pltpu.make_async_copy(qs, qall.at[pl.ds(k * rows, rows)], q_recv).start()
 
+    send_kv(0)
     send_kv(1)
     send_kv(2)
 

time: 49.2 us -> 48.9 us (level)
  the two profiles are of different devices: /device:TPU:26 before, /device:TPU:16 now
where the time goes in v4:
time: 48.9 us; the launch traced here: 48.6 us
  Pallas kernels  46.9 us (96%)
  matrix products  1.69 us (3%)
    pallas_call x1, Pallas kernels, shards(): pl.pallas_call(functools.partial(main_kernel, pbn, kan), out_shape=(jax.S...  27.3 us
    pallas_call x1, Pallas kernels, shards(): pl.pallas_call(functools.partial(reduce_kernel, pbn, kan), out_shape=jax....  18.6 us
    dot_general x1, matrix products, shards(): return jnp.dot(att, w_out, preferred_element_type=F32).astype(BF16)  1.69 us
    pallas_call x1, Pallas kernels, shards(): pl.pallas_call(functools.partial(redo_kernel, tiles, pbn), out_shape=(jax...  0.99 us

profile of v4, /device:TPU:16, one launch (start us, length us, event | category | flops | bytes accessed | tf_op | source)
XLA Modules:
  0.0 48.6 jit_solution(7595826906325359187)
XLA Ops:
  0.0 0.0 copy-start
  0.0 27.3 %gather_attend.1 = (bf16[512,256]{1,0:T(8,128)(2,1)}, bf16[4,16,128]{2,1,0:T(8,128)(2,1)}, s32[8,128]{1,0:T(8,128)}, bf16[512,256]{1,0:T(8,128)(2,1)}, bf16[2560,512]{1,0:T(8,128)(2,1)}) custom-call(f32[2,32]{1,0:T(2,128)} %pin_ref.3, f32[2,32]{1,0:T(2,128)} %psh_ref.3, f32[2,32]{1,0:T(2,128)} %pout_ref.3, bf16[64,1536]{1,0:T(8,128)(2,1)} %x_hbm.1, ...), custom_call_target="tpu_custom_call" | custom-call | tf_op jit(solution)/shard_map/gather_attend/pallas_call | solution.py:633
  27.3 1.0 %redo.1 = (bf16[512,256]{1,0:T(8,128)(2,1)}, bf16[4,16,128]{2,1,0:T(8,128)(2,1)}) custom-call(s32[1]{0:T(128)} %bitcast.start_ref, s32[8,128]{1,0:T(8,128)} %get-tuple-element.12.odd_ref, f32[2,32]{1,0:T(2,128)} %pin_ref.3, f32[2,32]{1,0:T(2,128)} %psh_ref.3, f32[2,32]{1,0:T(2,128)} %pout_ref.3, ...), custom_call_target="tpu_custom_call", output_to_operand_aliasing={{0}: (8, {}), {1}: (9, {})} | custom-call | tf_op jit(solution)/shard_map/redo/pallas_call | solution.py:677
  28.3 18.6 %reduce_rows.1 = bf16[64,256]{1,0:T(8,128)(2,1)} custom-call(bf16[512,256]{1,0:T(8,128)(2,1)} %get-tuple-element.17.num_ref, bf16[4,16,128]{2,1,0:T(8,128)(2,1)} %get-tuple-element.18.stat_ref), custom_call_target="tpu_custom_call" | custom-call | tf_op jit(solution)/shard_map/reduce_rows/pallas_call | solution.py:702
  46.9 0.0 copy-done
  46.9 1.7 %convolution_convert_fusion = bf16[64,1536]{1,0:T(8,128)(2,1)} fusion(bf16[64,256]{1,0:T(8,128)(2,1)} %reduce_rows.1, bf16[256,1536]{1,0:T(8,128)(2,1)S(1)} %copy-done), kind=kOutput, calls=%fused_computation | convolution fusion | flops 50429952 | bytes 1015808 | tf_op jit(solution)/shard_map/dot_general | solution.py:718
Async XLA Ops:
  0.0 46.9 %copy-start = (bf16[256,1536]{1,0:T(8,128)(2,1)S(1)}, bf16[256,1536]{1,0:T(8,128)(2,1)}, u32[]{:S(2)}) copy-start(bf16[256,1536]{1,0:T(8,128)(2,1)} %param.15) | copy-start | bytes 2359300
